TPU v7x, 256 devices: a whole 4x4x8 slice. The times are simulated.
256 devices in a mesh: blk: 256 (over x, z, y, core).
Axes of the slice: x: 4, y: 4, z: 8, core: 2. Of those that a mesh axis runs over, the one named last changes fastest.
Arguments:
- traces: bfloat16 [32768, 144, 128], P('blk')
- bands: int32 [64], replicated, may hold values from 0 to 7, never falling along the last dimension, each value on 1 to 16 neighbouring positions
Outputs:
- cross_spectra: bfloat16 [32768, 2, 2, 64, 128], P('blk')
Inputs may be any that keep to these rules, and one draw needn't show every extreme that they name: `bands`: band numbers never fall along the bins; every band holds 1 to 16 bins and one holds exactly 16.
All inputs are finite; a program needn't handle non-finite values.
Results may differ from a plain program's by a relative error of at most 0.024.
Values may be sent and summed in bfloat16 or wider, within the bound.
A program may use at most 128 MiB of HBM per device.

v0:
```python
import math

import jax
import jax.numpy as jnp
from jax import lax
from jax.sharding import PartitionSpec as P

HW = 16
RAM_HALF = 64
ROUNDS = 2


epsilon = 1e-05
floor_power = 0.25


def with_halo(cells, sides, width):
    for axis, dim in sides:
        count = lax.axis_size(axis)
        ends = count - 1
        head = lax.slice_in_dim(cells, 0, width, axis=dim)
        tail = lax.slice_in_dim(cells, cells.shape[dim] - width, cells.shape[dim], axis=dim)
        cells = jnp.concatenate(
            [
                lax.ppermute(tail, axis, [(i, (i + 1) % count) for i in range(ends)]),
                cells,
                lax.ppermute(head, axis, [((i + 1) % count, i) for i in range(ends)]),
            ],
            axis=dim,
        )
    return cells


def shifted(shard, axis, by):
    count = lax.axis_size(axis)
    return lax.ppermute(shard, axis, [(i, (i + by) % count) for i in range(count)])


def prepare(extended, first_channel, total_channels, bands, halo_width, ram_half):
    channel_count = extended.shape[0] - 2 * halo_width
    ext_rows = extended.shape[0]
    window_count = extended.shape[1]
    samples = extended.shape[2]
    bin_count = samples // 2
    inner = jnp.arange(channel_count, dtype=jnp.int32)
    outer = jnp.arange(ext_rows, dtype=jnp.int32)
    offset = outer[None, :] - inner[:, None]
    outer_position = first_channel - halo_width + outer
    inside = (outer_position >= 0) & (outer_position < total_channels)
    selector = (offset >= 0) & (offset <= 2 * halo_width) & inside[None, :]
    neighbour_count = jnp.sum(selector.astype(jnp.float32), axis=1)
    neighbour_sum = jnp.einsum(
        "ie,ewl->iwl", selector.astype(jnp.bfloat16), extended, preferred_element_type=jnp.float32
    )
    centred = (
        extended[halo_width : halo_width + channel_count].astype(jnp.float32)
        - neighbour_sum / neighbour_count[:, None, None]
    )
    balanced = centred.astype(jnp.bfloat16)
    magnitude = jnp.abs(balanced)
    sample_index = jnp.arange(samples, dtype=jnp.int32)
    ram_band = jnp.abs(sample_index[:, None] - sample_index[None, :]) <= ram_half
    ram_count = jnp.sum(ram_band.astype(jnp.float32), axis=0)
    ram_sum = jnp.einsum(
        "cwl,lm->cwm", magnitude, ram_band.astype(jnp.bfloat16), preferred_element_type=jnp.float32
    )
    envelope = ram_sum / ram_count + epsilon
    normalized = (balanced.astype(jnp.float32) / envelope).astype(jnp.bfloat16)
    frequency = jnp.arange(1, bin_count + 1, dtype=jnp.int32)
    phase_steps = frequency[:, None] * sample_index[None, :] % samples
    phase = 2.0 * math.pi / samples * phase_steps.astype(jnp.float32)
    dft_table = (
        jnp.concatenate([jnp.cos(phase), -jnp.sin(phase)], axis=0) / math.sqrt(samples)
    ).astype(jnp.bfloat16)
    spectra = jnp.einsum("jl,cwl->jwc", dft_table, normalized, preferred_element_type=jnp.float32)
    spectra = spectra.reshape(2, bin_count, window_count, channel_count)
    power_bins = spectra[0] * spectra[0] + spectra[1] * spectra[1]
    same_band = (bands[:, None] == bands[None, :]).astype(jnp.float32)
    band_matrix = same_band / jnp.sum(same_band, axis=1, keepdims=True)
    band_mean = jnp.einsum("fg,gwc->fwc", band_matrix, power_bins, precision=lax.Precision.HIGHEST)
    whiten_scale = lax.rsqrt(jnp.maximum(band_mean, floor_power))
    return (spectra * whiten_scale[None]).astype(jnp.bfloat16)


def correlate(own_block, partner):
    flipped = jnp.stack([jnp.stack([partner[0], partner[1]]), jnp.stack([-partner[1], partner[0]])])
    window_count = own_block.shape[2]
    product = jnp.einsum("kfwc,okfwd->cofd", own_block, flipped, preferred_element_type=jnp.float32)
    return (product / math.sqrt(window_count)).astype(jnp.bfloat16)


def per_device(traces, bands):
    extended = with_halo(traces, (("blk", 0),), HW)
    channel_count = traces.shape[0]
    block_count = lax.axis_size("blk")
    first_channel = lax.axis_index("blk") * channel_count
    own_block = prepare(extended, first_channel, channel_count * block_count, bands, HW, RAM_HALF)
    results = []
    for round_index in range(ROUNDS):
        partner = shifted(own_block, "blk", -(round_index + 1))
        results.append(correlate(own_block, partner))
    return jnp.stack(results, axis=1)


def solution(mesh):
    placed = (P("blk", None, None), P())
    return jax.shard_map(
        per_device,
        mesh=mesh,
        in_specs=placed,
        out_specs=P("blk", None, None, None, None),
        check_vma=False,
    )
```

profile of v0, /device:TPU:6, one launch (start us, length us, event | category | flops | bytes accessed | tf_op | source)
XLA Modules:
  0.0 261.7 jit_solution(5080897295654867422)
XLA Ops:
  0.0 0.0 copy-start.2
  0.0 3.6 %copy.12 = bf16[128,144,128]{2,0,1:T(8,128)(2,1)S(1)} copy(bf16[128,144,128]{2,1,0:T(8,128)(2,1)} %param.2) | data formatting | bytes 9437184 | tf_op args[0]
  3.6 0.0 copy-start
  3.6 2.2 copy-done
  5.8 0.2 fusion.76
  6.0 1.9 collective-permute-start
  7.9 9.9 %collective-permute-start.1 = (bf16[16,144,128]{2,0,1:T(8,128)(2,1)S(1)}, bf16[16,144,128]{2,0,1:T(8,128)(2,1)S(1)}, u32[]{:S(2)}, u32[]{:S(2)}) collective-permute-start(bf16[16,144,128]{2,0,1:T(8,128)(2,1)S(1)} %get-tuple-element.10), channel_id=1, source_target_pairs={{1,0},{2,1},{3,2},{4,3},{5,4},{6,5},{7,6},{8,7},{9,8},{10,9},{11,1... | collective-permute-start | bytes 1769480 | tf_op jit(solution)/shard_map/ppermute | solution.py:27
  17.9 0.0 copy-done.2
  17.9 0.2 convert_reduce_fusion.2
  18.1 0.1 convert_reduce_fusion
  18.2 0.2 fusion.63
  18.4 5.0 %collective-permute-done = bf16[16,144,128]{2,0,1:T(8,128)(2,1)S(1)} collective-permute-done((bf16[16,144,128]{2,0,1:T(8,128)(2,1)S(1)}, bf16[16,144,128]{2,0,1:T(8,128)(2,1)S(1)}, u32[]{:S(2)}, u32[]{:S(2)}) %collective-permute-start) | collective-permute-done | bytes 589856 | tf_op jit(solution)/shard_map/ppermute | solution.py:25
  23.5 1.8 collective-permute-done.1
  25.2 7.5 %fusion.9 = f32[128,144,128]{2,0,1:T(8,128)} fusion(bf16[16,144,128]{2,0,1:T(8,128)(2,1)S(1)} %collective-permute-done.1, bf16[128,144,128]{2,0,1:T(8,128)(2,1)} %copy-done, bf16[16,144,128]{2,0,1:T(8,128)(2,1)S(1)} %collective-permute-done, pred[160]{0:T(512)(128)(4,1)S(1)} %compare_and_fusion), kind=kOutput, calls=%fused_computation.16 | convolution fusion | flops 772771840 | bytes 15335584 | tf_op jit(solution)/shard_map/ie,ewl->iwl/dot_general | solution.py:52
  32.7 15.9 %fusion.22 = f32[128,144,128]{0,2,1:T(8,128)} fusion(f32[128]{0:T(128)S(1)} %convert_reduce_fusion.1, f32[128,144,128]{2,0,1:T(8,128)} %fusion.9, f32[128]{0:T(128)S(1)} %convert_reduce_fusion, f32[64,128]{1,0:T(8,128)S(1)} %get-tuple-element.12, f32[64,128]{1,0:T(8,128)S(1)} %get-tuple-element.11, bf16[128,144,128]{2,1,0:T(8,128)(2,1)} %param.2), kind=kOutput, calls=%fused_computation.33 | convolution fusion | flops 1241088000 | bytes 23659520 | tf_op jit(solution)/shard_map/jl,cwl->jwc/dot_general | solution.py:75
  48.6 7.0 %maximum_rsqrt_fusion = f32[64,144,128]{2,0,1:T(8,128)S(1)} fusion(f32[128,144,128]{2,0,1:T(8,128)} %bitcast.57, f32[64]{0:T(128)S(1)} %convert_reduce_fusion.2, s32[64]{0:T(128)S(1)} %copy-done.2), kind=kOutput, calls=%fused_computation.30 | convolution fusion | flops 910700544 | bytes 14157312 | tf_op jit(solution)/shard_map/fg,gwc->fwc/dot_general | solution.py:80
  55.7 2.7 %copy.16 = f32[64,144,128]{2,1,0:T(8,128)S(1)} copy(f32[64,144,128]{2,0,1:T(8,128)S(1)} %maximum_rsqrt_fusion) | data formatting | bytes 9437184 | tf_op jit(solution)/shard_map/rsqrt | solution.py:81
  58.4 12.0 %fusion.6 = bf16[2,64,144,128]{3,2,0,1:T(8,128)(2,1)} fusion(f32[2,64,144,128]{3,1,0,2:T(8,128)} %bitcast.58, f32[64,144,128]{2,1,0:T(8,128)S(1)} %copy.16), kind=kLoop, calls=%fused_computation.8 | loop fusion | flops 4718592 | bytes 18874368 | tf_op jit(solution)/shard_map/convert_element_type | solution.py:82
  70.4 2.3 collective-permute-start.3
  72.7 3.9 %collective-permute-start.2 = (bf16[2,64,144,128]{3,2,0,1:T(8,128)(2,1)}, bf16[2,64,144,128]{3,2,0,1:T(8,128)(2,1)}, u32[]{:S(2)}, u32[]{:S(2)}) collective-permute-start(bf16[2,64,144,128]{3,2,0,1:T(8,128)(2,1)} %fusion.6), channel_id=1, source_target_pairs={{0,255},{1,0},{2,1},{3,2},{4,3},{5,4},{6,5},{7,6},{8,7},{9,8},{10,... | collective-permute-start | bytes 14155784 | tf_op jit(solution)/shard_map/ppermute | solution.py:36
  76.6 95.3 %collective-permute-done.3 = bf16[2,64,144,128]{3,2,0,1:T(8,128)(2,1)S(1)} collective-permute-done((bf16[2,64,144,128]{3,2,0,1:T(8,128)(2,1)}, bf16[2,64,144,128]{3,2,0,1:T(8,128)(2,1)S(1)}, u32[]{:S(2)}, u32[]{:S(2)}) %collective-permute-start.3) | collective-permute-done | bytes 4718624 | tf_op jit(solution)/shard_map/ppermute | solution.py:36
  171.9 0.0 copy-start.1
  171.9 0.5 slice_negate_fusion
  172.4 1.8 copy-done.1
  174.2 2.6 maximum_bitcast_fusion.1
  176.7 10.7 %fusion.24 = bf16[128,1,2,64,128]{0,4,2,3,1:T(8,128)(2,1)} fusion(bf16[2,64,144,128]{3,2,0,1:T(8,128)(2,1)} %fusion.6, bf16[1,2,64,144,128]{4,3,1,2,0:T(8,128)(2,1)} %maximum_bitcast_fusion.1, bf16[1,2,64,144,128]{4,3,1,2,0:T(8,128)(2,1)} %bitcast.59), kind=kOutput, calls=%fused_computation.35 | convolution fusion | flops 1216872448 | bytes 18350080 | tf_op jit(solution)/shard_map/kfwc,okfwd->cofd/dot_general | solution.py:88
  187.5 38.3 %collective-permute-done.2 = bf16[2,64,144,128]{3,2,0,1:T(8,128)(2,1)} collective-permute-done((bf16[2,64,144,128]{3,2,0,1:T(8,128)(2,1)}, bf16[2,64,144,128]{3,2,0,1:T(8,128)(2,1)}, u32[]{:S(2)}, u32[]{:S(2)}) %collective-permute-start.2) | collective-permute-done | bytes 4718624 | tf_op jit(solution)/shard_map/ppermute | solution.py:36
  225.8 2.8 %slice_negate_fusion.1 = (bf16[1,64,144,128]{3,2,0,1:T(8,128)(2,1)S(1)}, bf16[1,64,144,128]{3,2,0,1:T(8,128)(2,1)S(1)}) fusion(bf16[2,64,144,128]{3,2,0,1:T(8,128)(2,1)} %collective-permute-done.2), kind=kLoop, calls=%fused_computation.37 | loop fusion | flops 1179648 | bytes 9437184 | tf_op jit(solution)/shard_map/neg | solution.py:86
  228.6 2.6 maximum_bitcast_fusion
  231.2 11.1 %fusion.23 = bf16[128,1,2,64,128]{0,4,2,3,1:T(8,128)(2,1)} fusion(bf16[2,64,144,128]{3,2,0,1:T(8,128)(2,1)} %fusion.6, bf16[1,2,64,144,128]{4,3,1,0,2:T(8,128)(2,1)} %maximum_bitcast_fusion, bf16[1,2,64,144,128]{4,3,1,0,2:T(8,128)(2,1)} %bitcast.7), kind=kOutput, calls=%fused_computation.34 | convolution fusion | flops 1216872448 | bytes 18350080 | tf_op jit(solution)/shard_map/kfwc,okfwd->cofd/dot_general | solution.py:88
  242.3 7.5 %pad_maximum_fusion.1 = bf16[128,2,2,64,128]{0,4,2,3,1:T(8,128)(2,1)} fusion(bf16[128,1,2,64,128]{0,4,2,3,1:T(8,128)(2,1)} %fusion.24, bf16[128,1,2,64,128]{0,4,2,3,1:T(8,128)(2,1)} %fusion.23), kind=kLoop, calls=%fused_computation.11 | loop fusion | flops 4194304 | bytes 16777216 | tf_op jit(solution)/shard_map/stack | solution.py:102
  249.8 11.9 %copy.20 = bf16[128,2,2,64,128]{4,3,2,1,0:T(8,128)(2,1)} copy(bf16[128,2,2,64,128]{0,4,2,3,1:T(8,128)(2,1)} %pad_maximum_fusion.1) | data formatting | bytes 16777216 | tf_op jit(solution)/shard_map/stack | solution.py:102
  (3 shorter events, 0.1 us)
Async XLA Ops:
  0.0 17.9 %copy-start.2 = (s32[64]{0:T(128)S(1)}, s32[64]{0:T(128)}, u32[]{:S(2)}) copy-start(s32[64]{0:T(128)} %param.3) | copy-start | bytes 772
  3.6 2.2 copy-start
  6.0 17.5 %collective-permute-start = (bf16[16,144,128]{2,0,1:T(8,128)(2,1)S(1)}, bf16[16,144,128]{2,0,1:T(8,128)(2,1)S(1)}, u32[]{:S(2)}, u32[]{:S(2)}) collective-permute-start(bf16[16,144,128]{2,0,1:T(8,128)(2,1)S(1)} %get-tuple-element.9), channel_id=1, source_target_pairs={{0,1},{1,2},{2,3},{3,4},{4,5},{5,6},{6,7},{7,8},{8,9},{9,10},{10,1... | collective-permute-start | bytes 1769480 | tf_op jit(solution)/shard_map/ppermute | solution.py:25
  7.9 17.3 %collective-permute-start.1 = (bf16[16,144,128]{2,0,1:T(8,128)(2,1)S(1)}, bf16[16,144,128]{2,0,1:T(8,128)(2,1)S(1)}, u32[]{:S(2)}, u32[]{:S(2)}) collective-permute-start(bf16[16,144,128]{2,0,1:T(8,128)(2,1)S(1)} %get-tuple-element.10), channel_id=1, source_target_pairs={{1,0},{2,1},{3,2},{4,3},{5,4},{6,5},{7,6},{8,7},{9,8},{10,9},{11,1... | collective-permute-start | bytes 1769480 | tf_op jit(solution)/shard_map/ppermute | solution.py:27
  70.4 101.5 %collective-permute-start.3 = (bf16[2,64,144,128]{3,2,0,1:T(8,128)(2,1)}, bf16[2,64,144,128]{3,2,0,1:T(8,128)(2,1)S(1)}, u32[]{:S(2)}, u32[]{:S(2)}) collective-permute-start(bf16[2,64,144,128]{3,2,0,1:T(8,128)(2,1)} %fusion.6), channel_id=1, source_target_pairs={{0,254},{1,255},{2,0},{3,1},{4,2},{5,3},{6,4},{7,5},{8,6},{9,7},{1... | collective-permute-start | bytes 14155784 | tf_op jit(solution)/shard_map/ppermute | solution.py:36
  72.7 153.1 %collective-permute-start.2 = (bf16[2,64,144,128]{3,2,0,1:T(8,128)(2,1)}, bf16[2,64,144,128]{3,2,0,1:T(8,128)(2,1)}, u32[]{:S(2)}, u32[]{:S(2)}) collective-permute-start(bf16[2,64,144,128]{3,2,0,1:T(8,128)(2,1)} %fusion.6), channel_id=1, source_target_pairs={{0,255},{1,0},{2,1},{3,2},{4,3},{5,4},{6,5},{7,6},{8,7},{9,8},{10,... | collective-permute-start | bytes 14155784 | tf_op jit(solution)/shard_map/ppermute | solution.py:36
  171.9 2.2 copy-start.1
where the time goes:
time: 262 us
  waiting for transfers between devices  140 us (53%)
  matrix products  52.2 us (20%)
  other arithmetic  28.5 us (11%)
  local copies, waits for them, and re-layouts  22.4 us (9%)
  starting transfers between devices  18 us (7%)
    ppermute x2, waiting for transfers between devices, shifted(): lax.ppermute(shard, axis, [(i, (i + by) % count) for i in range(count)])  134 us
    dot_general x2, matrix products, correlate(): jnp.einsum('kfwc,okfwd->cofd', own_block, flipped, preferred_element_type...  21.8 us
    dot_general x1, matrix products, prepare(): jnp.einsum('jl,cwl->jwc', dft_table, normalized, preferred_element_type=j...  15.9 us
    convert_element_type x1, other arithmetic, prepare(): return (spectra * whiten_scale[None]).astype(jnp.bfloat16)  12 us
    another operation x1, local copies, waits for them, and re-layouts, per_device(): return jnp.stack(results, axis=1)  11.9 us
    ppermute x1, starting transfers between devices, with_halo(): lax.ppermute(head, axis, [((i + 1) % count, i) for i in range(ends)])  9.92 us
    unnamed x7, local copies, waits for them, and re-layouts  7.56 us
    dot_general x1, matrix products, prepare(): jnp.einsum('ie,ewl->iwl', selector.astype(jnp.bfloat16), extended, prefer...  7.47 us
  transfers between devices with their start and end apart: 4, of which 4 were waited for; matrix products, arithmetic and copies ran while one was open for 5% of the time, Pallas kernels for 0%

commit v1 on v0

--- a/solution.py
+++ b/solution.py
@@ -95,10 +95,11 @@
     block_count = lax.axis_size("blk")
     first_channel = lax.axis_index("blk") * channel_count
     own_block = prepare(extended, first_channel, channel_count * block_count, bands, HW, RAM_HALF)
-    results = []
-    for round_index in range(ROUNDS):
-        partner = shifted(own_block, "blk", -(round_index + 1))
-        results.append(correlate(own_block, partner))
+    second = shifted(own_block, "blk", -2)
+    pairs_up = [(2 * i + 1, 2 * i) for i in range(block_count // 2)]
+    pairs_down = [(2 * i, 2 * i + 1) for i in range(block_count // 2)]
+    first = lax.ppermute(own_block, "blk", pairs_up) + lax.ppermute(second, "blk", pairs_down)
+    results = [correlate(own_block, first), correlate(own_block, second)]
     return jnp.stack(results, axis=1)
 
 

time: 262 us -> 236 us (0.901)
  waiting for transfers between devices: 140 us -> 105 us
  starting transfers between devices: 18 us -> 23 us
  other arithmetic: 28.5 us -> 33.4 us
    ppermute x2 -> x1, waiting for transfers between devices: 134 us -> 97.9 us  [shifted(): lax.ppermute(shard, axis, [(i, (i + by) % count) for i in range(count)])]
    ppermute x0 -> x2, starting transfers between devices: none -> 8.88 us  [the longest x1 7.6 us: per_device(): lax.ppermute(second, 'blk', pairs_down)]
    add x0 -> x1, other arithmetic: none -> 4.99 us  [per_device(): lax.ppermute(own_block, 'blk', pairs_up)]
    ppermute x2 -> x1, starting transfers between devices: 6.15 us -> 2.29 us  [shifted(): lax.ppermute(shard, axis, [(i, (i + by) % count) for i in range(count)])]
  transfers between devices with their start and end apart: 4 -> 5, of which waited for: 4 -> 3; matrix products, arithmetic and copies ran while one was open for 5% -> 7% of each run, Pallas kernels for 0% -> 0%
where the time goes in v1:
time: 236 us
  waiting for transfers between devices  105 us (44%)
  matrix products  52.3 us (22%)
  other arithmetic  33.4 us (14%)
  starting transfers between devices  23 us (10%)
  local copies, waits for them, and re-layouts  22.3 us (9%)
    ppermute x1, waiting for transfers between devices, shifted(): lax.ppermute(shard, axis, [(i, (i + by) % count) for i in range(count)])  97.9 us
    dot_general x2, matrix products, correlate(): jnp.einsum('kfwc,okfwd->cofd', own_block, flipped, preferred_element_type...  21.9 us
    dot_general x1, matrix products, prepare(): jnp.einsum('jl,cwl->jwc', dft_table, normalized, preferred_element_type=j...  16 us
    convert_element_type x1, other arithmetic, prepare(): return (spectra * whiten_scale[None]).astype(jnp.bfloat16)  12 us
    another operation x1, local copies, waits for them, and re-layouts, per_device(): return jnp.stack(results, axis=1)  11.9 us
    ppermute x1, starting transfers between devices, with_halo(): lax.ppermute(head, axis, [((i + 1) % count, i) for i in range(ends)])  9.92 us
    ppermute x1, starting transfers between devices, per_device(): lax.ppermute(second, 'blk', pairs_down)  7.6 us
    unnamed x7, local copies, waits for them, and re-layouts  7.47 us
  transfers between devices with their start and end apart: 5, of which 3 were waited for; matrix products, arithmetic and copies ran while one was open for 7% of the time, Pallas kernels for 0%

profile of v1, /device:TPU:6, one launch (start us, length us, event | category | flops | bytes accessed | tf_op | source)
XLA Modules:
  0.0 235.8 jit_solution(11061773641306515911)
XLA Ops:
  0.0 0.0 copy-start.2
  0.0 3.6 %copy.12 = bf16[128,144,128]{2,0,1:T(8,128)(2,1)S(1)} copy(bf16[128,144,128]{2,1,0:T(8,128)(2,1)} %param.2) | data formatting | bytes 9437184 | tf_op args[0]
  3.6 0.0 copy-start.1
  3.6 2.2 copy-done.1
  5.8 0.2 fusion.76
  6.0 1.9 collective-permute-start
  7.9 9.9 %collective-permute-start.1 = (bf16[16,144,128]{2,0,1:T(8,128)(2,1)S(1)}, bf16[16,144,128]{2,0,1:T(8,128)(2,1)S(1)}, u32[]{:S(2)}, u32[]{:S(2)}) collective-permute-start(bf16[16,144,128]{2,0,1:T(8,128)(2,1)S(1)} %get-tuple-element.10), channel_id=1, source_target_pairs={{1,0},{2,1},{3,2},{4,3},{5,4},{6,5},{7,6},{8,7},{9,8},{10,9},{11,1... | collective-permute-start | bytes 1769480 | tf_op jit(solution)/shard_map/ppermute | solution.py:27
  17.9 0.0 copy-done.2
  17.9 0.2 convert_reduce_fusion.2
  18.1 0.1 convert_reduce_fusion
  18.2 0.2 fusion.63
  18.4 5.0 %collective-permute-done = bf16[16,144,128]{2,0,1:T(8,128)(2,1)S(1)} collective-permute-done((bf16[16,144,128]{2,0,1:T(8,128)(2,1)S(1)}, bf16[16,144,128]{2,0,1:T(8,128)(2,1)S(1)}, u32[]{:S(2)}, u32[]{:S(2)}) %collective-permute-start) | collective-permute-done | bytes 589856 | tf_op jit(solution)/shard_map/ppermute | solution.py:25
  23.5 1.8 collective-permute-done.1
  25.2 7.5 %fusion.9 = f32[128,144,128]{2,0,1:T(8,128)} fusion(bf16[16,144,128]{2,0,1:T(8,128)(2,1)S(1)} %collective-permute-done.1, bf16[128,144,128]{2,0,1:T(8,128)(2,1)} %copy-done.1, bf16[16,144,128]{2,0,1:T(8,128)(2,1)S(1)} %collective-permute-done, pred[160]{0:T(512)(128)(4,1)S(1)} %compare_and_fusion), kind=kOutput, calls=%fused_computation.16 | convolution fusion | flops 772771840 | bytes 15335584 | tf_op jit(solution)/shard_map/ie,ewl->iwl/dot_general | solution.py:52
  32.7 16.0 %fusion.22 = f32[128,144,128]{0,2,1:T(8,128)} fusion(f32[128]{0:T(128)S(1)} %convert_reduce_fusion.1, f32[128,144,128]{2,0,1:T(8,128)} %fusion.9, f32[128]{0:T(128)S(1)} %convert_reduce_fusion, f32[64,128]{1,0:T(8,128)S(1)} %get-tuple-element.12, f32[64,128]{1,0:T(8,128)S(1)} %get-tuple-element.11, bf16[128,144,128]{2,1,0:T(8,128)(2,1)} %param.2), kind=kOutput, calls=%fused_computation.33 | convolution fusion | flops 1241088000 | bytes 23659520 | tf_op jit(solution)/shard_map/jl,cwl->jwc/dot_general | solution.py:75
  48.7 7.0 %maximum_rsqrt_fusion = f32[64,144,128]{2,0,1:T(8,128)S(1)} fusion(f32[128,144,128]{2,0,1:T(8,128)} %bitcast.57, f32[64]{0:T(128)S(1)} %convert_reduce_fusion.2, s32[64]{0:T(128)S(1)} %copy-done.2), kind=kOutput, calls=%fused_computation.30 | convolution fusion | flops 910700544 | bytes 14157312 | tf_op jit(solution)/shard_map/fg,gwc->fwc/dot_general | solution.py:80
  55.7 2.7 %copy.16 = f32[64,144,128]{2,1,0:T(8,128)S(1)} copy(f32[64,144,128]{2,0,1:T(8,128)S(1)} %maximum_rsqrt_fusion) | data formatting | bytes 9437184 | tf_op jit(solution)/shard_map/rsqrt | solution.py:81
  58.5 12.0 %fusion.6 = bf16[2,64,144,128]{3,2,0,1:T(8,128)(2,1)} fusion(f32[2,64,144,128]{3,1,0,2:T(8,128)} %bitcast.58, f32[64,144,128]{2,1,0:T(8,128)S(1)} %copy.16), kind=kLoop, calls=%fused_computation.8 | loop fusion | flops 4718592 | bytes 18874368 | tf_op jit(solution)/shard_map/convert_element_type | solution.py:82
  70.5 2.3 collective-permute-start.3
  72.8 1.3 collective-permute-start.2
  74.0 97.9 %collective-permute-done.3 = bf16[2,64,144,128]{3,2,0,1:T(8,128)(2,1)} collective-permute-done((bf16[2,64,144,128]{3,2,0,1:T(8,128)(2,1)}, bf16[2,64,144,128]{3,2,0,1:T(8,128)(2,1)}, u32[]{:S(2)}, u32[]{:S(2)}) %collective-permute-start.3) | collective-permute-done | bytes 4718624 | tf_op jit(solution)/shard_map/ppermute | solution.py:36
  171.9 7.6 %collective-permute-start.4 = (bf16[2,64,144,128]{3,2,0,1:T(8,128)(2,1)}, bf16[2,64,144,128]{3,2,0,1:T(8,128)(2,1)}, u32[]{:S(2)}, u32[]{:S(2)}) collective-permute-start(bf16[2,64,144,128]{3,2,0,1:T(8,128)(2,1)} %collective-permute-done.3), channel_id=1, source_target_pairs={{0,1},{2,3},{4,5},{6,7},{8,9},{10,11},{12,13},{14,15},{16,17},{18,... | collective-permute-start | bytes 14155784 | tf_op jit(solution)/shard_map/ppermute | solution.py:101
  179.5 2.8 %slice_negate_fusion = (bf16[1,64,144,128]{3,2,0,1:T(8,128)(2,1)S(1)}, bf16[1,64,144,128]{3,2,0,1:T(8,128)(2,1)S(1)}) fusion(bf16[2,64,144,128]{3,2,0,1:T(8,128)(2,1)} %collective-permute-done.3), kind=kLoop, calls=%fused_computation.36 | loop fusion | flops 1179648 | bytes 9437184 | tf_op jit(solution)/shard_map/neg | solution.py:86
  182.4 2.5 %maximum_bitcast_fusion.1 = bf16[1,2,64,144,128]{4,3,1,2,0:T(8,128)(2,1)} fusion(bf16[1,64,144,128]{3,2,0,1:T(8,128)(2,1)S(1)} %get-tuple-element.8, bf16[1,64,144,128]{3,2,0,1:T(8,128)(2,1)S(1)} %get-tuple-element.7), kind=kLoop, calls=%fused_computation.27 | loop fusion | flops 2359296 | bytes 9437184 | tf_op jit(solution)/shard_map/stack | solution.py:86
  184.9 10.8 %fusion.24 = bf16[128,1,2,64,128]{0,4,2,3,1:T(8,128)(2,1)} fusion(bf16[2,64,144,128]{3,2,0,1:T(8,128)(2,1)} %fusion.6, bf16[1,2,64,144,128]{4,3,1,2,0:T(8,128)(2,1)} %maximum_bitcast_fusion.1, bf16[1,2,64,144,128]{4,3,1,2,0:T(8,128)(2,1)} %bitcast.15), kind=kOutput, calls=%fused_computation.35 | convolution fusion | flops 1216872448 | bytes 18350080 | tf_op jit(solution)/shard_map/kfwc,okfwd->cofd/dot_general | solution.py:88
  195.7 0.0 collective-permute-done.2
  195.7 0.0 collective-permute-done.4
  195.7 5.0 %add.51 = bf16[2,64,144,128]{3,2,0,1:T(8,128)(2,1)S(1)} add(bf16[2,64,144,128]{3,2,0,1:T(8,128)(2,1)} %collective-permute-done.2, bf16[2,64,144,128]{3,2,0,1:T(8,128)(2,1)} %collective-permute-done.4) | non-fusion elementwise | flops 2359296 | bytes 14155776 | tf_op jit(solution)/shard_map/add | solution.py:101
  200.7 0.0 copy-start
  200.7 0.5 slice_negate_fusion.1
  201.2 1.7 copy-done
  202.9 2.5 %maximum_bitcast_fusion = bf16[1,2,64,144,128]{4,3,1,0,2:T(8,128)(2,1)} fusion(bf16[1,64,144,128]{3,2,0,1:T(8,128)(2,1)S(1)} %get-tuple-element.6, bf16[1,64,144,128]{3,2,0,1:T(8,128)(2,1)S(1)} %get-tuple-element.5), kind=kLoop, calls=%fused_computation.26 | loop fusion | flops 2359296 | bytes 9437184 | tf_op jit(solution)/shard_map/stack | solution.py:86
  205.4 11.1 %fusion.23 = bf16[128,1,2,64,128]{0,4,2,3,1:T(8,128)(2,1)} fusion(bf16[2,64,144,128]{3,2,0,1:T(8,128)(2,1)} %fusion.6, bf16[1,2,64,144,128]{4,3,1,0,2:T(8,128)(2,1)} %maximum_bitcast_fusion, bf16[1,2,64,144,128]{4,3,1,0,2:T(8,128)(2,1)} %bitcast.59), kind=kOutput, calls=%fused_computation.34 | convolution fusion | flops 1216872448 | bytes 18350080 | tf_op jit(solution)/shard_map/kfwc,okfwd->cofd/dot_general | solution.py:88
  216.5 7.5 %pad_maximum_fusion.1 = bf16[128,2,2,64,128]{0,4,2,3,1:T(8,128)(2,1)} fusion(bf16[128,1,2,64,128]{0,4,2,3,1:T(8,128)(2,1)} %fusion.24, bf16[128,1,2,64,128]{0,4,2,3,1:T(8,128)(2,1)} %fusion.23), kind=kLoop, calls=%fused_computation.11 | loop fusion | flops 4194304 | bytes 16777216 | tf_op jit(solution)/shard_map/stack | solution.py:103
  223.9 11.9 %copy.20 = bf16[128,2,2,64,128]{4,3,2,1,0:T(8,128)(2,1)} copy(bf16[128,2,2,64,128]{0,4,2,3,1:T(8,128)(2,1)} %pad_maximum_fusion.1) | data formatting | bytes 16777216 | tf_op jit(solution)/shard_map/stack | solution.py:103
  (3 shorter events, 0.1 us)
Async XLA Ops:
  0.0 17.9 %copy-start.2 = (s32[64]{0:T(128)S(1)}, s32[64]{0:T(128)}, u32[]{:S(2)}) copy-start(s32[64]{0:T(128)} %param.3) | copy-start | bytes 772
  3.6 2.2 copy-start.1
  6.0 17.5 %collective-permute-start = (bf16[16,144,128]{2,0,1:T(8,128)(2,1)S(1)}, bf16[16,144,128]{2,0,1:T(8,128)(2,1)S(1)}, u32[]{:S(2)}, u32[]{:S(2)}) collective-permute-start(bf16[16,144,128]{2,0,1:T(8,128)(2,1)S(1)} %get-tuple-element.9), channel_id=1, source_target_pairs={{0,1},{1,2},{2,3},{3,4},{4,5},{5,6},{6,7},{7,8},{8,9},{9,10},{10,1... | collective-permute-start | bytes 1769480 | tf_op jit(solution)/shard_map/ppermute | solution.py:25
  7.9 17.3 %collective-permute-start.1 = (bf16[16,144,128]{2,0,1:T(8,128)(2,1)S(1)}, bf16[16,144,128]{2,0,1:T(8,128)(2,1)S(1)}, u32[]{:S(2)}, u32[]{:S(2)}) collective-permute-start(bf16[16,144,128]{2,0,1:T(8,128)(2,1)S(1)} %get-tuple-element.10), channel_id=1, source_target_pairs={{1,0},{2,1},{3,2},{4,3},{5,4},{6,5},{7,6},{8,7},{9,8},{10,9},{11,1... | collective-permute-start | bytes 1769480 | tf_op jit(solution)/shard_map/ppermute | solution.py:27
  70.5 101.5 %collective-permute-start.3 = (bf16[2,64,144,128]{3,2,0,1:T(8,128)(2,1)}, bf16[2,64,144,128]{3,2,0,1:T(8,128)(2,1)}, u32[]{:S(2)}, u32[]{:S(2)}) collective-permute-start(bf16[2,64,144,128]{3,2,0,1:T(8,128)(2,1)} %fusion.6), channel_id=1, source_target_pairs={{0,254},{1,255},{2,0},{3,1},{4,2},{5,3},{6,4},{7,5},{8,6},{9,7},{1... | collective-permute-start | bytes 14155784 | tf_op jit(solution)/shard_map/ppermute | solution.py:36
  72.8 122.9 %collective-permute-start.2 = (bf16[2,64,144,128]{3,2,0,1:T(8,128)(2,1)}, bf16[2,64,144,128]{3,2,0,1:T(8,128)(2,1)}, u32[]{:S(2)}, u32[]{:S(2)}) collective-permute-start(bf16[2,64,144,128]{3,2,0,1:T(8,128)(2,1)} %fusion.6), channel_id=1, source_target_pairs={{1,0},{3,2},{5,4},{7,6},{9,8},{11,10},{13,12},{15,14},{17,16},{19,... | collective-permute-start | bytes 14155784 | tf_op jit(solution)/shard_map/ppermute | solution.py:101
  171.9 23.7 %collective-permute-start.4 = (bf16[2,64,144,128]{3,2,0,1:T(8,128)(2,1)}, bf16[2,64,144,128]{3,2,0,1:T(8,128)(2,1)}, u32[]{:S(2)}, u32[]{:S(2)}) collective-permute-start(bf16[2,64,144,128]{3,2,0,1:T(8,128)(2,1)} %collective-permute-done.3), channel_id=1, source_target_pairs={{0,1},{2,3},{4,5},{6,7},{8,9},{10,11},{12,13},{14,15},{16,17},{18,... | collective-permute-start | bytes 14155784 | tf_op jit(solution)/shard_map/ppermute | solution.py:101
  200.7 2.2 copy-start

commit v2 on v0

--- a/solution.py
+++ b/solution.py
@@ -1,9 +1,14 @@
+import functools
 import math
 
 import jax
 import jax.numpy as jnp
 from jax import lax
+from jax.experimental import pallas as pl
+from jax.experimental.pallas import tpu as pltpu
 from jax.sharding import PartitionSpec as P
+
+MESH = pl.DeviceIdType.MESH
 
 HW = 16
 RAM_HALF = 64
@@ -82,11 +87,98 @@
     return (spectra * whiten_scale[None]).astype(jnp.bfloat16)
 
 
-def correlate(own_block, partner):
-    flipped = jnp.stack([jnp.stack([partner[0], partner[1]]), jnp.stack([-partner[1], partner[0]])])
-    window_count = own_block.shape[2]
-    product = jnp.einsum("kfwc,okfwd->cofd", own_block, flipped, preferred_element_type=jnp.float32)
-    return (product / math.sqrt(window_count)).astype(jnp.bfloat16)
+def correlate_chunk(own, partner, out, r, rows, scale):
+    real_rows, imag_rows = [], []
+    for j in range(rows.size):
+        f = rows.start + j
+        x = own[:, f]
+        y = partner[:, f]
+        lhs = x.reshape(-1, x.shape[-1])
+        real_rhs = y.reshape(-1, y.shape[-1])
+        imag_rhs = jnp.concatenate([-y[1], y[0]], axis=0)
+        dims = (((0,), (0,)), ((), ()))
+        real = lax.dot_general(lhs, real_rhs, dims, preferred_element_type=jnp.float32)
+        imag = lax.dot_general(lhs, imag_rhs, dims, preferred_element_type=jnp.float32)
+        real_rows.append(real / scale)
+        imag_rows.append(imag / scale)
+    out[:, r, 0, rows, :] = jnp.stack(real_rows, axis=1).astype(out.dtype)
+    out[:, r, 1, rows, :] = jnp.stack(imag_rows, axis=1).astype(out.dtype)
+
+
+def exchange_kernel(n, chunks, scale, own, out, first, second, first_send, first_recv, second_send, second_recv):
+    me = lax.axis_index("blk")
+    core = lax.rem(me, 2)
+    down = lax.rem(me + n - 2, n)
+    up = lax.rem(me + 2, n)
+    mate = me + 1 - 2 * core
+
+    barrier = pltpu.get_barrier_semaphore()
+    for peer in (down, up, mate):
+        pl.semaphore_signal(barrier, inc=1, device_id=(peer,), device_id_type=MESH)
+    pl.semaphore_wait(barrier, 3)
+
+    size = own.shape[1] // chunks
+
+    def part(i):
+        return pl.ds(pl.multiple_of(i * size, size), size)
+
+    def to_down(i):
+        return pltpu.make_async_remote_copy(
+            own.at[:, part(i)], second.at[:, part(i)], second_send.at[i], second_recv.at[i],
+            device_id=(down,), device_id_type=MESH)
+
+    def to_mate(src, i):
+        return pltpu.make_async_remote_copy(
+            src.at[:, part(i)], first.at[:, part(i)], first_send.at[i], first_recv.at[i],
+            device_id=(mate,), device_id_type=MESH)
+
+    @pl.loop(0, chunks)
+    def _(i):
+        to_down(i).start()
+
+    @pl.when(core == 1)
+    def _():
+        @pl.loop(0, chunks)
+        def _(i):
+            to_mate(own, i).start()
+
+    @pl.loop(0, chunks)
+    def _(i):
+        to_down(i).wait_recv()
+
+        @pl.when(core == 0)
+        def _():
+            to_mate(second, i).start()
+
+        correlate_chunk(own, second, out, 1, part(i), scale)
+        to_mate(second, i).wait_recv()
+        correlate_chunk(own, first, out, 0, part(i), scale)
+
+    @pl.loop(0, chunks)
+    def _(i):
+        to_down(i).wait_send()
+        to_mate(second, i).wait_send()
+
+
+def exchange(own_block, chunks=4):
+    n = lax.axis_size("blk")
+    parts, bins, windows, channels = own_block.shape
+    out_shape = jax.ShapeDtypeStruct((channels, ROUNDS, 2, bins, channels), jnp.bfloat16)
+    return pl.pallas_call(
+        functools.partial(exchange_kernel, n, chunks, math.sqrt(windows)),
+        out_shape=out_shape,
+        in_specs=[pl.BlockSpec(memory_space=pltpu.VMEM)],
+        out_specs=pl.BlockSpec(memory_space=pltpu.VMEM),
+        scratch_shapes=[
+            pltpu.VMEM(own_block.shape, own_block.dtype),
+            pltpu.VMEM(own_block.shape, own_block.dtype),
+            pltpu.SemaphoreType.DMA((chunks,)),
+            pltpu.SemaphoreType.DMA((chunks,)),
+            pltpu.SemaphoreType.DMA((chunks,)),
+            pltpu.SemaphoreType.DMA((chunks,)),
+        ],
+        compiler_params=pltpu.CompilerParams(collective_id=0, has_side_effects=True),
+    )(own_block)
 
 
 def per_device(traces, bands):
@@ -95,11 +187,7 @@
     block_count = lax.axis_size("blk")
     first_channel = lax.axis_index("blk") * channel_count
     own_block = prepare(extended, first_channel, channel_count * block_count, bands, HW, RAM_HALF)
-    results = []
-    for round_index in range(ROUNDS):
-        partner = shifted(own_block, "blk", -(round_index + 1))
-        results.append(correlate(own_block, partner))
-    return jnp.stack(results, axis=1)
+    return exchange(own_block)
 
 
 def solution(mesh):

time: 262 us -> 202 us (0.77); the launches traced: 262 us -> 199 us
  waiting for transfers between devices: 140 us -> 6.79 us
  Pallas kernels: 0 us -> 111 us
  matrix products: 52.2 us -> 28.6 us
  other arithmetic: 28.5 us -> 7.33 us
  local copies, waits for them, and re-layouts: 22.4 us -> 32.7 us
  starting transfers between devices: 18 us -> 11.8 us
    ppermute x2 -> x0, waiting for transfers between devices: 134 us -> none  [shifted(): lax.ppermute(shard, axis, [(i, (i + by) % count) for i in range(count)])]
    pallas_call x0 -> x1, Pallas kernels: none -> 111 us  [exchange(): pl.pallas_call(functools.partial(exchange_kernel, n, chunks, math.sqrt(wi...]
    dot_general x2 -> x0, matrix products: 21.8 us -> none  [correlate(): jnp.einsum('kfwc,okfwd->cofd', own_block, flipped, preferred_element_type...]
    transpose x0 -> x1, local copies, waits for them, and re-layouts: none -> 12.9 us  [prepare(): jnp.einsum('jl,cwl->jwc', dft_table, normalized, preferred_element_type=j...]
    another operation x3 -> x0, other arithmetic: 12.6 us -> none  [the longest x1 7.46 us: per_device(): return jnp.stack(results, axis=1)]
    another operation x1 -> x0, local copies, waits for them, and re-layouts: 11.9 us -> none  [per_device(): return jnp.stack(results, axis=1)]
    unnamed x7 -> x8, local copies, waits for them, and re-layouts: 7.56 us -> 16.6 us
    ppermute x2 -> x0, starting transfers between devices: 6.15 us -> none  [shifted(): lax.ppermute(shard, axis, [(i, (i + by) % count) for i in range(count)])]
  transfers between devices with their start and end apart: 4 -> 2, of which waited for: 4 -> 2; matrix products, arithmetic and copies ran while one was open for 5% -> 0% of each run, Pallas kernels for 0% -> 0%
where the time goes in v2:
time: 202 us; the launch traced here: 199 us
  Pallas kernels  111 us (55%)
  local copies, waits for them, and re-layouts  32.7 us (16%)
  matrix products  28.6 us (14%)
  starting transfers between devices  11.8 us (6%)
  other arithmetic  7.33 us (4%)
  waiting for transfers between devices  6.79 us (3%)
    pallas_call x1, Pallas kernels, exchange(): pl.pallas_call(functools.partial(exchange_kernel, n, chunks, math.sqrt(wi...  111 us
    unnamed x8, local copies, waits for them, and re-layouts  16.6 us
    dot_general x1, matrix products, prepare(): jnp.einsum('jl,cwl->jwc', dft_table, normalized, preferred_element_type=j...  16.3 us
    transpose x1, local copies, waits for them, and re-layouts, prepare(): jnp.einsum('jl,cwl->jwc', dft_table, normalized, preferred_element_type=j...  12.9 us
    ppermute x1, starting transfers between devices, with_halo(): lax.ppermute(head, axis, [((i + 1) % count, i) for i in range(ends)])  9.92 us
    dot_general x1, matrix products, prepare(): jnp.einsum('ie,ewl->iwl', selector.astype(jnp.bfloat16), extended, prefer...  7.5 us
    convert_element_type x1, other arithmetic, prepare(): return (spectra * whiten_scale[None]).astype(jnp.bfloat16)  6.77 us
    ppermute x1, waiting for transfers between devices, with_halo(): lax.ppermute(tail, axis, [(i, (i + 1) % count) for i in range(ends)])  5.04 us
  transfers between devices with their start and end apart: 2, of which 2 were waited for; matrix products, arithmetic and copies ran while one was open for 0% of the time, Pallas kernels for 0%

profile of v2, /device:TPU:6, one launch (start us, length us, event | category | flops | bytes accessed | tf_op | source)
XLA Modules:
  0.0 198.5 jit_solution(12410692726864930050)
XLA Ops:
  0.0 0.0 copy-start.2
  0.0 3.6 %copy.9 = bf16[128,144,128]{2,0,1:T(8,128)(2,1)S(1)} copy(bf16[128,144,128]{2,1,0:T(8,128)(2,1)} %param.2) | data formatting | bytes 9437184 | tf_op args[0]
  3.6 0.0 copy-start.1
  3.6 2.2 %copy-done.1 = bf16[128,144,128]{2,0,1:T(8,128)(2,1)} copy-done((bf16[128,144,128]{2,0,1:T(8,128)(2,1)}, bf16[128,144,128]{2,0,1:T(8,128)(2,1)S(1)}, u32[]{:S(2)}) %copy-start.1) | copy-done | bytes 4718616
  5.8 0.2 fusion.57
  6.0 1.9 collective-permute-start
  7.9 9.9 %collective-permute-start.1 = (bf16[16,144,128]{2,0,1:T(8,128)(2,1)S(1)}, bf16[16,144,128]{2,0,1:T(8,128)(2,1)S(1)}, u32[]{:S(2)}, u32[]{:S(2)}) collective-permute-start(bf16[16,144,128]{2,0,1:T(8,128)(2,1)S(1)} %get-tuple-element.6), channel_id=1, source_target_pairs={{1,0},{2,1},{3,2},{4,3},{5,4},{6,5},{7,6},{8,7},{9,8},{10,9},{11,1... | collective-permute-start | bytes 1769480 | tf_op jit(solution)/shard_map/ppermute | solution.py:32
  17.9 0.0 copy-done.2
  17.9 0.2 convert_reduce_fusion.2
  18.1 0.1 convert_reduce_fusion
  18.2 0.2 fusion.45
  18.4 5.0 %collective-permute-done = bf16[16,144,128]{2,0,1:T(8,128)(2,1)S(1)} collective-permute-done((bf16[16,144,128]{2,0,1:T(8,128)(2,1)S(1)}, bf16[16,144,128]{2,0,1:T(8,128)(2,1)S(1)}, u32[]{:S(2)}, u32[]{:S(2)}) %collective-permute-start) | collective-permute-done | bytes 589856 | tf_op jit(solution)/shard_map/ppermute | solution.py:30
  23.5 1.8 collective-permute-done.1
  25.2 7.5 %fusion = f32[128,144,128]{2,0,1:T(8,128)} fusion(bf16[16,144,128]{2,0,1:T(8,128)(2,1)S(1)} %collective-permute-done.1, bf16[128,144,128]{2,0,1:T(8,128)(2,1)} %copy-done.1, bf16[16,144,128]{2,0,1:T(8,128)(2,1)S(1)} %collective-permute-done, pred[160]{0:T(512)(128)(4,1)S(1)} %compare_and_fusion), kind=kOutput, calls=%fused_computation.3 | convolution fusion | flops 772771840 | bytes 15335584 | tf_op jit(solution)/shard_map/ie,ewl->iwl/dot_general | solution.py:57
  32.7 16.3 %fusion.16 = f32[128,144,128]{2,0,1:T(8,128)} fusion(f32[128]{0:T(128)S(1)} %convert_reduce_fusion.1, f32[128,144,128]{2,0,1:T(8,128)} %fusion, f32[128]{0:T(128)S(1)} %convert_reduce_fusion, f32[64,128]{1,0:T(8,128)S(1)} %get-tuple-element.8, f32[64,128]{1,0:T(8,128)S(1)} %get-tuple-element.7, bf16[128,144,128]{2,1,0:T(8,128)(2,1)} %param.2), kind=kOutput, calls=%fused_computation.17 | convolution fusion | flops 1241088000 | bytes 23659520 | tf_op jit(solution)/shard_map/jl,cwl->jwc/dot_general | solution.py:80
  49.0 0.0 copy-start
  49.1 12.9 %copy.13 = f32[128,144,128]{2,1,0:T(8,128)} copy(f32[128,144,128]{2,0,1:T(8,128)} %fusion.16) | data formatting | bytes 18874368 | tf_op jit(solution)/shard_map/jl,cwl->jwc/transpose | solution.py:80
  62.0 0.0 copy-done
  62.0 4.8 %maximum_rsqrt_fusion = f32[64,144,128]{2,0,1:T(8,128)S(1)} fusion(f32[128,144,128]{2,0,1:T(8,128)S(1)} %copy-done, f32[64]{0:T(128)S(1)} %convert_reduce_fusion.2, s32[64]{0:T(128)S(1)} %copy-done.2), kind=kOutput, calls=%fused_computation.13 | convolution fusion | flops 910700544 | bytes 14157312 | tf_op jit(solution)/shard_map/fg,gwc->fwc/dot_general | solution.py:85
  66.8 3.0 %copy.14 = f32[64,144,128]{2,1,0:T(8,128)S(1)} copy(f32[64,144,128]{2,0,1:T(8,128)S(1)} %maximum_rsqrt_fusion) | data formatting | bytes 9437184 | tf_op jit(solution)/shard_map/rsqrt | solution.py:86
  69.8 6.8 %multiply_convert_fusion.own = bf16[2,64,144,128]{3,2,1,0:T(8,128)(2,1)} fusion(f32[2,64,144,128]{3,2,1,0:T(8,128)} %bitcast.16, f32[64,144,128]{2,1,0:T(8,128)S(1)} %copy.14), kind=kLoop, calls=%fused_computation | loop fusion | flops 4718592 | bytes 18874368 | tf_op jit(solution)/shard_map/convert_element_type | solution.py:87
  76.5 111.2 %shard_map.28 = bf16[128,2,2,64,128]{4,3,2,1,0:T(8,128)(2,1)} custom-call(bf16[2,64,144,128]{3,2,1,0:T(8,128)(2,1)} %multiply_convert_fusion.own), custom_call_target="tpu_custom_call" | custom-call | tf_op jit(solution)/shard_map/pallas_call | solution.py:167
  187.7 10.8 %copy.24 = bf16[128,2,2,64,128]{4,3,2,1,0:T(8,128)(2,1)} copy(bf16[128,2,2,64,128]{4,3,2,1,0:T(8,128)(2,1)} %shard_map.28) | data formatting | bytes 16777216
  (3 shorter events, 0.1 us)
Async XLA Ops:
  0.0 17.9 %copy-start.2 = (s32[64]{0:T(128)S(1)}, s32[64]{0:T(128)}, u32[]{:S(2)}) copy-start(s32[64]{0:T(128)} %param.3) | copy-start | bytes 772
  3.6 2.2 %copy-start.1 = (bf16[128,144,128]{2,0,1:T(8,128)(2,1)}, bf16[128,144,128]{2,0,1:T(8,128)(2,1)S(1)}, u32[]{:S(2)}) copy-start(bf16[128,144,128]{2,0,1:T(8,128)(2,1)S(1)} %copy.9) | copy-start | bytes 14155780
  6.0 17.5 %collective-permute-start = (bf16[16,144,128]{2,0,1:T(8,128)(2,1)S(1)}, bf16[16,144,128]{2,0,1:T(8,128)(2,1)S(1)}, u32[]{:S(2)}, u32[]{:S(2)}) collective-permute-start(bf16[16,144,128]{2,0,1:T(8,128)(2,1)S(1)} %get-tuple-element.5), channel_id=1, source_target_pairs={{0,1},{1,2},{2,3},{3,4},{4,5},{5,6},{6,7},{7,8},{8,9},{9,10},{10,1... | collective-permute-start | bytes 1769480 | tf_op jit(solution)/shard_map/ppermute | solution.py:30
  7.9 17.3 %collective-permute-start.1 = (bf16[16,144,128]{2,0,1:T(8,128)(2,1)S(1)}, bf16[16,144,128]{2,0,1:T(8,128)(2,1)S(1)}, u32[]{:S(2)}, u32[]{:S(2)}) collective-permute-start(bf16[16,144,128]{2,0,1:T(8,128)(2,1)S(1)} %get-tuple-element.6), channel_id=1, source_target_pairs={{1,0},{2,1},{3,2},{4,3},{5,4},{6,5},{7,6},{8,7},{9,8},{10,9},{11,1... | collective-permute-start | bytes 1769480 | tf_op jit(solution)/shard_map/ppermute | solution.py:32
  49.0 13.0 %copy-start = (f32[128,144,128]{2,0,1:T(8,128)S(1)}, f32[128,144,128]{2,0,1:T(8,128)}, u32[]{:S(2)}) copy-start(f32[128,144,128]{2,0,1:T(8,128)} %fusion.16) | copy-start | bytes 28311556

commit v3 on v2

--- a/solution.py
+++ b/solution.py
@@ -181,12 +181,95 @@
     )(own_block)
 
 
+def prepare_kernel(ext_ref, sel_ref, count_ref, ram_ref, ram_count_ref, table_ref, band_ref, out_ref):
+    halo = (ext_ref.shape[0] - sel_ref.shape[0]) // 2
+    channels = sel_ref.shape[0]
+    bins = band_ref.shape[0]
+    block = jnp.swapaxes(ext_ref[...].astype(jnp.float32), 0, 1)
+    sel = sel_ref[...]
+    count = count_ref[...]
+    ram = ram_ref[...]
+    ram_count = ram_count_ref[...]
+    table = table_ref[...]
+    band = band_ref[...]
+    rows = []
+    for w in range(block.shape[0]):
+        x = block[w]
+        neighbour_sum = jnp.dot(sel, x.astype(jnp.bfloat16), preferred_element_type=jnp.float32)
+        balanced = (x[halo : halo + channels] - neighbour_sum / count).astype(jnp.bfloat16)
+        ram_sum = jnp.dot(jnp.abs(balanced), ram, preferred_element_type=jnp.float32)
+        envelope = ram_sum / ram_count + epsilon
+        normalized = (balanced.astype(jnp.float32) / envelope).astype(jnp.bfloat16)
+        spectra = lax.dot_general(
+            table, normalized, (((1,), (1,)), ((), ())), preferred_element_type=jnp.float32
+        )
+        real, imag = spectra[:bins], spectra[bins:]
+        power = real * real + imag * imag
+        band_mean = jnp.dot(band, power, precision=lax.Precision.HIGHEST, preferred_element_type=jnp.float32)
+        scale = lax.rsqrt(jnp.maximum(band_mean, floor_power))
+        rows.append(jnp.concatenate([real * scale, imag * scale], axis=0))
+    whitened = jnp.swapaxes(jnp.stack(rows, axis=0), 0, 1).astype(out_ref.dtype)
+    out_ref[0] = whitened[:bins]
+    out_ref[1] = whitened[bins:]
+
+
+def prepare_fast(extended, first_channel, total_channels, bands, halo_width, ram_half, windows_per_step=16):
+    channel_count = extended.shape[0] - 2 * halo_width
+    ext_rows = extended.shape[0]
+    window_count = extended.shape[1]
+    samples = extended.shape[2]
+    bin_count = samples // 2
+    inner = jnp.arange(channel_count, dtype=jnp.int32)
+    outer = jnp.arange(ext_rows, dtype=jnp.int32)
+    offset = outer[None, :] - inner[:, None]
+    outer_position = first_channel - halo_width + outer
+    inside = (outer_position >= 0) & (outer_position < total_channels)
+    selector = (offset >= 0) & (offset <= 2 * halo_width) & inside[None, :]
+    neighbour_count = jnp.sum(selector.astype(jnp.float32), axis=1)[:, None]
+    sample_index = jnp.arange(samples, dtype=jnp.int32)
+    ram_band = jnp.abs(sample_index[:, None] - sample_index[None, :]) <= ram_half
+    ram_count = jnp.sum(ram_band.astype(jnp.float32), axis=0)[None, :]
+    frequency = jnp.arange(1, bin_count + 1, dtype=jnp.int32)
+    phase_steps = frequency[:, None] * sample_index[None, :] % samples
+    phase = 2.0 * math.pi / samples * phase_steps.astype(jnp.float32)
+    dft_table = (
+        jnp.concatenate([jnp.cos(phase), -jnp.sin(phase)], axis=0) / math.sqrt(samples)
+    ).astype(jnp.bfloat16)
+    same_band = (bands[:, None] == bands[None, :]).astype(jnp.float32)
+    band_matrix = same_band / jnp.sum(same_band, axis=1, keepdims=True)
+    step = windows_per_step
+    whole = lambda i: (0, 0)
+    return pl.pallas_call(
+        prepare_kernel,
+        out_shape=jax.ShapeDtypeStruct((2, bin_count, window_count, channel_count), jnp.bfloat16),
+        grid=(window_count // step,),
+        in_specs=[
+            pl.BlockSpec((ext_rows, step, samples), lambda i: (0, i, 0)),
+            pl.BlockSpec((channel_count, ext_rows), whole),
+            pl.BlockSpec((channel_count, 1), whole),
+            pl.BlockSpec((samples, samples), whole),
+            pl.BlockSpec((1, samples), whole),
+            pl.BlockSpec((samples, samples), whole),
+            pl.BlockSpec((bin_count, bin_count), whole),
+        ],
+        out_specs=pl.BlockSpec((2, bin_count, step, channel_count), lambda i: (0, 0, i, 0)),
+    )(
+        extended,
+        selector.astype(jnp.bfloat16),
+        neighbour_count,
+        ram_band.astype(jnp.bfloat16),
+        ram_count,
+        dft_table,
+        band_matrix,
+    )
+
+
 def per_device(traces, bands):
     extended = with_halo(traces, (("blk", 0),), HW)
     channel_count = traces.shape[0]
     block_count = lax.axis_size("blk")
     first_channel = lax.axis_index("blk") * channel_count
-    own_block = prepare(extended, first_channel, channel_count * block_count, bands, HW, RAM_HALF)
+    own_block = prepare_fast(extended, first_channel, channel_count * block_count, bands, HW, RAM_HALF)
     return exchange(own_block)
 
 

time: 202 us -> 206 us (1.020)
  Pallas kernels: 111 us -> 165 us
  matrix products: 28.6 us -> 0 us
  local copies, waits for them, and re-layouts: 32.7 us -> 12.8 us
  waiting for transfers between devices: 6.79 us -> 1.52 us
  other arithmetic: 7.33 us -> 11 us
    pallas_call x0 -> x1, Pallas kernels: none -> 53.5 us  [prepare_fast(): pl.pallas_call(prepare_kernel, out_shape=jax.ShapeDtypeStruct((2, bin_cou...]
    dot_general x3 -> x0, matrix products: 28.6 us -> none  [the longest x1 16.3 us: prepare(): jnp.einsum('jl,cwl->jwc', dft_table, normalized, preferred_element_type=j...]
    transpose x1 -> x0, local copies, waits for them, and re-layouts: 12.9 us -> none  [prepare(): jnp.einsum('jl,cwl->jwc', dft_table, normalized, preferred_element_type=j...]
    concatenate x0 -> x1, other arithmetic: none -> 5.86 us  [with_halo(): jnp.concatenate([lax.ppermute(tail, axis, [(i, (i + 1) % count) for i in...]
    unnamed x8 -> x1, local copies, waits for them, and re-layouts: 16.6 us -> 10.8 us
    ppermute x1, waiting for transfers between devices: 5.04 us -> 0.01 us  [with_halo(): lax.ppermute(tail, axis, [(i, (i + 1) % count) for i in range(ends)])]
    convert_element_type x1 -> x3, other arithmetic: 6.77 us -> 1.88 us  [the longest x1 0.65 us: prepare_fast(): selector.astype(jnp.bfloat16)]
    rsqrt x1 -> x0, local copies, waits for them, and re-layouts: 2.95 us -> none  [prepare(): whiten_scale = lax.rsqrt(jnp.maximum(band_mean, floor_power))]
  transfers between devices with their start and end apart: 2 -> 2, of which waited for: 2 -> 1; matrix products, arithmetic and copies ran while one was open for 0% -> 3% of each run, Pallas kernels for 0% -> 0%
where the time goes in v3:
time: 206 us; the launch traced here: 202 us
  Pallas kernels  165 us (80%)
  local copies, waits for them, and re-layouts  12.8 us (6%)
  starting transfers between devices  11.8 us (6%)
  other arithmetic  11 us (5%)
    pallas_call x1, Pallas kernels, exchange(): pl.pallas_call(functools.partial(exchange_kernel, n, chunks, math.sqrt(wi...  111 us
    pallas_call x1, Pallas kernels, prepare_fast(): pl.pallas_call(prepare_kernel, out_shape=jax.ShapeDtypeStruct((2, bin_cou...  53.5 us
    unnamed x1, local copies, waits for them, and re-layouts  10.8 us
    ppermute x1, starting transfers between devices, with_halo(): lax.ppermute(head, axis, [((i + 1) % count, i) for i in range(ends)])  9.92 us
    concatenate x1, other arithmetic, with_halo(): jnp.concatenate([lax.ppermute(tail, axis, [(i, (i + 1) % count) for i in...  5.86 us
  transfers between devices with their start and end apart: 2, of which 1 were waited for; matrix products, arithmetic and copies ran while one was open for 3% of the time, Pallas kernels for 0%

profile of v3, /device:TPU:6, one launch (start us, length us, event | category | flops | bytes accessed | tf_op | source)
XLA Modules:
  0.0 201.9 jit_solution(7595503072587129887)
XLA Ops:
  0.0 1.3 fusion.14
  1.3 1.9 collective-permute-start
  3.3 9.9 %collective-permute-start.1 = (bf16[16,144,128]{2,1,0:T(8,128)(2,1)S(1)}, bf16[16,144,128]{2,1,0:T(8,128)(2,1)S(1)}, u32[]{:S(2)}, u32[]{:S(2)}) collective-permute-start(bf16[16,144,128]{2,1,0:T(8,128)(2,1)S(1)} %get-tuple-element.6), channel_id=1, source_target_pairs={{1,0},{2,1},{3,2},{4,3},{5,4},{6,5},{7,6},{8,7},{9,8},{10,9},{11,1... | collective-permute-start | bytes 1769480 | tf_op jit(solution)/shard_map/ppermute | solution.py:32
  13.2 0.6 fusion.6.ram_ref
  13.8 0.1 convert_reduce_fusion
  13.9 0.2 fusion.13
  14.2 0.6 fusion.4.table_ref
  14.8 0.7 copy.3.count_ref
  15.5 0.6 convert_reduce_fusion.1
  16.1 0.9 convert_reduce_fusion.2
  17.0 1.4 convert_divide_fusion.band_ref
  18.4 0.6 fusion.5.sel_ref
  19.0 0.0 collective-permute-done
  19.0 1.5 collective-permute-done.1
  20.6 5.9 %pad_maximum_fusion.ext_ref = bf16[160,144,128]{2,1,0:T(8,128)(2,1)} fusion(bf16[16,144,128]{2,1,0:T(8,128)(2,1)S(1)} %collective-permute-done.1, bf16[128,144,128]{2,1,0:T(8,128)(2,1)} %param.2, bf16[16,144,128]{2,1,0:T(8,128)(2,1)S(1)} %collective-permute-done), kind=kLoop, calls=%fused_computation | loop fusion | flops 5898240 | bytes 11796480 | tf_op jit(solution)/shard_map/concatenate | solution.py:28
  26.4 53.5 %shard_map.28.own = bf16[2,64,144,128]{3,2,1,0:T(8,128)(2,1)} custom-call(bf16[160,144,128]{2,1,0:T(8,128)(2,1)} %pad_maximum_fusion.ext_ref, bf16[128,160]{1,0:T(8,128)(2,1)} %fusion.5.sel_ref, f32[128,1]{1,0:T(8,128)} %copy.3.count_ref, bf16[128,128]{1,0:T(8,128)(2,1)} %fusion.6.ram_ref, f32[1,128]{1,0:T(1,128)} %bitcast.2, ...), custom_call_target="tpu_custom_call" | custom-call | tf_op jit(solution)/shard_map/pallas_call | solution.py:242
  79.9 111.2 %shard_map.29 = bf16[128,2,2,64,128]{4,3,2,1,0:T(8,128)(2,1)} custom-call(bf16[2,64,144,128]{3,2,1,0:T(8,128)(2,1)} %shard_map.28.own), custom_call_target="tpu_custom_call" | custom-call | tf_op jit(solution)/shard_map/pallas_call | solution.py:167
  191.1 10.8 %copy.5 = bf16[128,2,2,64,128]{4,3,2,1,0:T(8,128)(2,1)} copy(bf16[128,2,2,64,128]{4,3,2,1,0:T(8,128)(2,1)} %shard_map.29) | data formatting | bytes 16777216
  (2 shorter events, 0.0 us)
Async XLA Ops:
  1.3 17.7 %collective-permute-start = (bf16[16,144,128]{2,1,0:T(8,128)(2,1)S(1)}, bf16[16,144,128]{2,1,0:T(8,128)(2,1)S(1)}, u32[]{:S(2)}, u32[]{:S(2)}) collective-permute-start(bf16[16,144,128]{2,1,0:T(8,128)(2,1)S(1)} %get-tuple-element.5), channel_id=1, source_target_pairs={{0,1},{1,2},{2,3},{3,4},{4,5},{5,6},{6,7},{7,8},{8,9},{9,10},{10,1... | collective-permute-start | bytes 1769480 | tf_op jit(solution)/shard_map/ppermute | solution.py:30
  3.3 17.3 %collective-permute-start.1 = (bf16[16,144,128]{2,1,0:T(8,128)(2,1)S(1)}, bf16[16,144,128]{2,1,0:T(8,128)(2,1)S(1)}, u32[]{:S(2)}, u32[]{:S(2)}) collective-permute-start(bf16[16,144,128]{2,1,0:T(8,128)(2,1)S(1)} %get-tuple-element.6), channel_id=1, source_target_pairs={{1,0},{2,1},{3,2},{4,3},{5,4},{6,5},{7,6},{8,7},{9,8},{10,9},{11,1... | collective-permute-start | bytes 1769480 | tf_op jit(solution)/shard_map/ppermute | solution.py:32

commit v4 on v0

--- a/solution.py
+++ b/solution.py
@@ -1,9 +1,14 @@
+import functools
 import math
 
 import jax
 import jax.numpy as jnp
 from jax import lax
+from jax.experimental import pallas as pl
+from jax.experimental.pallas import tpu as pltpu
 from jax.sharding import PartitionSpec as P
+
+MESH = pl.DeviceIdType.MESH
 
 HW = 16
 RAM_HALF = 64
@@ -82,24 +87,203 @@
     return (spectra * whiten_scale[None]).astype(jnp.bfloat16)
 
 
-def correlate(own_block, partner):
-    flipped = jnp.stack([jnp.stack([partner[0], partner[1]]), jnp.stack([-partner[1], partner[0]])])
-    window_count = own_block.shape[2]
-    product = jnp.einsum("kfwc,okfwd->cofd", own_block, flipped, preferred_element_type=jnp.float32)
-    return (product / math.sqrt(window_count)).astype(jnp.bfloat16)
-
-
-def per_device(traces, bands):
+def whiten_block(block, sel, count, ram, ram_count, table, band):
+    halo = (block.shape[0] - sel.shape[0]) // 2
+    channels = sel.shape[0]
+    bins = band.shape[0]
+    block = jnp.swapaxes(block.astype(jnp.float32), 0, 1)
+    rows = []
+    for w in range(block.shape[0]):
+        x = block[w]
+        neighbour_sum = jnp.dot(sel, x.astype(jnp.bfloat16), preferred_element_type=jnp.float32)
+        balanced = (x[halo : halo + channels] - neighbour_sum / count).astype(jnp.bfloat16)
+        ram_sum = jnp.dot(jnp.abs(balanced), ram, preferred_element_type=jnp.float32)
+        envelope = ram_sum / ram_count + epsilon
+        normalized = (balanced.astype(jnp.float32) / envelope).astype(jnp.bfloat16)
+        spectra = lax.dot_general(
+            table, normalized, (((1,), (1,)), ((), ())), preferred_element_type=jnp.float32
+        )
+        real, imag = spectra[:bins], spectra[bins:]
+        power = real * real + imag * imag
+        band_mean = jnp.dot(band, power, precision=lax.Precision.HIGHEST, preferred_element_type=jnp.float32)
+        scale = lax.rsqrt(jnp.maximum(band_mean, floor_power))
+        rows.append(jnp.concatenate([real * scale, imag * scale], axis=0))
+    whitened = jnp.swapaxes(jnp.stack(rows, axis=0), 0, 1)
+    return whitened.reshape(2, bins, whitened.shape[1], channels)
+
+
+def prepare_kernel(ext_ref, sel_ref, count_ref, ram_ref, ram_count_ref, table_ref, band_ref, out_ref):
+    consts = [r[...] for r in (sel_ref, count_ref, ram_ref, ram_count_ref, table_ref, band_ref)]
+    out_ref[...] = whiten_block(ext_ref[...], *consts).astype(out_ref.dtype)
+
+
+def constants(first_channel, total_channels, bands, channel_count, halo_width, samples, ram_half):
+    ext_rows = channel_count + 2 * halo_width
+    bin_count = samples // 2
+    inner = jnp.arange(channel_count, dtype=jnp.int32)
+    outer = jnp.arange(ext_rows, dtype=jnp.int32)
+    offset = outer[None, :] - inner[:, None]
+    outer_position = first_channel - halo_width + outer
+    inside = (outer_position >= 0) & (outer_position < total_channels)
+    selector = (offset >= 0) & (offset <= 2 * halo_width) & inside[None, :]
+    neighbour_count = jnp.sum(selector.astype(jnp.float32), axis=1)[:, None]
+    sample_index = jnp.arange(samples, dtype=jnp.int32)
+    ram_band = jnp.abs(sample_index[:, None] - sample_index[None, :]) <= ram_half
+    ram_count = jnp.sum(ram_band.astype(jnp.float32), axis=0)[None, :]
+    frequency = jnp.arange(1, bin_count + 1, dtype=jnp.int32)
+    phase_steps = frequency[:, None] * sample_index[None, :] % samples
+    phase = 2.0 * math.pi / samples * phase_steps.astype(jnp.float32)
+    dft_table = (
+        jnp.concatenate([jnp.cos(phase), -jnp.sin(phase)], axis=0) / math.sqrt(samples)
+    ).astype(jnp.bfloat16)
+    same_band = (bands[:, None] == bands[None, :]).astype(jnp.float32)
+    band_matrix = same_band / jnp.sum(same_band, axis=1, keepdims=True)
+    return [
+        selector.astype(jnp.bfloat16),
+        neighbour_count,
+        ram_band.astype(jnp.bfloat16),
+        ram_count,
+        dft_table,
+        band_matrix,
+    ]
+
+
+def prepare_fast(extended, consts, windows, step=16):
+    ext_rows, _, samples = extended.shape
+    channel_count = consts[0].shape[0]
+    bin_count = samples // 2
+    whole = lambda i: (0, 0)
+    return pl.pallas_call(
+        prepare_kernel,
+        out_shape=jax.ShapeDtypeStruct((2, bin_count, windows, channel_count), jnp.bfloat16),
+        grid=(windows // step,),
+        in_specs=[pl.BlockSpec((ext_rows, step, samples), lambda i: (0, i, 0))]
+        + [pl.BlockSpec(c.shape, whole) for c in consts],
+        out_specs=pl.BlockSpec((2, bin_count, step, channel_count), lambda i: (0, 0, i, 0)),
+    )(extended, *consts)
+
+
+def correlate_chunk(owns, partners, out, r, rows, scale):
+    dims = (((0,), (0,)), ((), ()))
+    real_rows, imag_rows = [], []
+    for j in range(rows.size):
+        f = rows.start + j
+        real, imag = 0.0, 0.0
+        for own, partner in zip(owns, partners):
+            x = own[:, f]
+            y = partner[:, f]
+            lhs = x.reshape(-1, x.shape[-1])
+            real_rhs = y.reshape(-1, y.shape[-1])
+            imag_rhs = jnp.concatenate([-y[1], y[0]], axis=0)
+            real = real + lax.dot_general(lhs, real_rhs, dims, preferred_element_type=jnp.float32)
+            imag = imag + lax.dot_general(lhs, imag_rhs, dims, preferred_element_type=jnp.float32)
+        real_rows.append(real / scale)
+        imag_rows.append(imag / scale)
+    out[:, r, 0, rows, :] = jnp.stack(real_rows, axis=1).astype(out.dtype)
+    out[:, r, 1, rows, :] = jnp.stack(imag_rows, axis=1).astype(out.dtype)
+
+
+def exchange_kernel(n, chunks, scale, step, early, ext, sel, count, ram, ram_count, table, band,
+                    out, late, first, second, first_send, first_recv, second_send, second_recv):
+    me = lax.axis_index("blk")
+    core = lax.rem(me, 2)
+    down = lax.rem(me + n - 2, n)
+    up = lax.rem(me + 2, n)
+    mate = me + 1 - 2 * core
+
+    barrier = pltpu.get_barrier_semaphore()
+    for peer in (down, up, mate):
+        pl.semaphore_signal(barrier, inc=1, device_id=(peer,), device_id_type=MESH)
+    pl.semaphore_wait(barrier, 3)
+
+    size = early.shape[1] // chunks
+    owns = (early, late)
+
+    def part(i):
+        return pl.ds(pl.multiple_of(i * size, size), size)
+
+    def to_down(p, i):
+        return pltpu.make_async_remote_copy(
+            owns[p].at[:, part(i)], second[p].at[:, part(i)], second_send.at[p, i], second_recv.at[p, i],
+            device_id=(down,), device_id_type=MESH)
+
+    def to_mate(src, p, i):
+        return pltpu.make_async_remote_copy(
+            src.at[:, part(i)], first[p].at[:, part(i)], first_send.at[p, i], first_recv.at[p, i],
+            device_id=(mate,), device_id_type=MESH)
+
+    def send_part(p):
+        @pl.loop(0, chunks)
+        def _(i):
+            to_down(p, i).start()
+
+        @pl.when(core == 1)
+        def _():
+            @pl.loop(0, chunks)
+            def _(i):
+                to_mate(owns[p], p, i).start()
+
+    send_part(0)
+
+    consts = [r[...] for r in (sel, count, ram, ram_count, table, band)]
+
+    @pl.loop(0, ext.shape[1] // step)
+    def _(b):
+        windows = pl.ds(pl.multiple_of(b * step, step), step)
+        late[:, :, windows, :] = whiten_block(ext[:, windows, :], *consts).astype(late.dtype)
+
+    send_part(1)
+
+    @pl.loop(0, chunks)
+    def _(i):
+        for p in range(2):
+            to_down(p, i).wait_recv()
+
+            @pl.when(core == 0)
+            def _():
+                to_mate(second[p], p, i).start()
+
+        correlate_chunk(owns, second, out, 1, part(i), scale)
+        for p in range(2):
+            to_mate(second[p], p, i).wait_recv()
+        correlate_chunk(owns, first, out, 0, part(i), scale)
+
+    @pl.loop(0, chunks)
+    def _(i):
+        for p in range(2):
+            to_down(p, i).wait_send()
+            to_mate(second[p], p, i).wait_send()
+
+
+def per_device(traces, bands, chunks=4, early_windows=64):
     extended = with_halo(traces, (("blk", 0),), HW)
-    channel_count = traces.shape[0]
-    block_count = lax.axis_size("blk")
+    channel_count, window_count, samples = traces.shape
+    n = lax.axis_size("blk")
     first_channel = lax.axis_index("blk") * channel_count
-    own_block = prepare(extended, first_channel, channel_count * block_count, bands, HW, RAM_HALF)
-    results = []
-    for round_index in range(ROUNDS):
-        partner = shifted(own_block, "blk", -(round_index + 1))
-        results.append(correlate(own_block, partner))
-    return jnp.stack(results, axis=1)
+    consts = constants(first_channel, channel_count * n, bands, channel_count, HW, samples, RAM_HALF)
+    early = prepare_fast(extended, consts, early_windows)
+    rest = extended[:, early_windows:]
+    bins = samples // 2
+    late_shape = (2, bins, window_count - early_windows, channel_count)
+    vmem = pl.BlockSpec(memory_space=pltpu.VMEM)
+    return pl.pallas_call(
+        functools.partial(exchange_kernel, n, chunks, math.sqrt(window_count), 16),
+        out_shape=jax.ShapeDtypeStruct((channel_count, ROUNDS, 2, bins, channel_count), jnp.bfloat16),
+        in_specs=[vmem] * 8,
+        out_specs=vmem,
+        scratch_shapes=[
+            pltpu.VMEM(late_shape, jnp.bfloat16),
+            [pltpu.VMEM(early.shape, jnp.bfloat16), pltpu.VMEM(late_shape, jnp.bfloat16)],
+            [pltpu.VMEM(early.shape, jnp.bfloat16), pltpu.VMEM(late_shape, jnp.bfloat16)],
+            pltpu.SemaphoreType.DMA((2, chunks)),
+            pltpu.SemaphoreType.DMA((2, chunks)),
+            pltpu.SemaphoreType.DMA((2, chunks)),
+            pltpu.SemaphoreType.DMA((2, chunks)),
+        ],
+        compiler_params=pltpu.CompilerParams(
+            collective_id=0, has_side_effects=True, vmem_limit_bytes=60 * 1024 * 1024
+        ),
+    )(early, rest, *consts)
 
 
 def solution(mesh):

time: 262 us -> 182 us (0.69)
  the two profiles are of different devices: /device:TPU:6 before, /device:TPU:249 now
where the time goes in v4:
time: 182 us
  Pallas kernels  145 us (80%)
  local copies, waits for them, and re-layouts  20.8 us (11%)
  starting transfers between devices  9.78 us (5%)
  other arithmetic  5.07 us (3%)
    pallas_call x1, Pallas kernels, per_device(): pl.pallas_call(functools.partial(exchange_kernel, n, chunks, math.sqrt(wi...  120 us
    pallas_call x1, Pallas kernels, prepare_fast(): pl.pallas_call(prepare_kernel, out_shape=jax.ShapeDtypeStruct((2, bin_cou...  24.8 us
    unnamed x5, local copies, waits for them, and re-layouts  16.3 us
    ppermute x1, starting transfers between devices, with_halo(): lax.ppermute(tail, axis, [(i, (i + 1) % count) for i in range(ends)])  7.2 us
  transfers between devices with their start and end apart: 2, of which 1 were waited for; matrix products, arithmetic and copies ran while one was open for 5% of the time, Pallas kernels for 0%

profile of v4, /device:TPU:249, one launch (start us, length us, event | category | flops | bytes accessed | tf_op | source)
XLA Modules:
  0.0 182.0 jit_solution(12586998838323786006)
XLA Ops:
  0.0 1.3 fusion.14
  1.3 2.6 %collective-permute-start.1 = (bf16[16,144,128]{2,1,0:T(8,128)(2,1)S(1)}, bf16[16,144,128]{2,1,0:T(8,128)(2,1)S(1)}, u32[]{:S(2)}, u32[]{:S(2)}) collective-permute-start(bf16[16,144,128]{2,1,0:T(8,128)(2,1)S(1)} %get-tuple-element.5), channel_id=1, source_target_pairs={{1,0},{2,1},{3,2},{4,3},{5,4},{6,5},{7,6},{8,7},{9,8},{10,9},{11,1... | collective-permute-start | bytes 1769480 | tf_op jit(solution)/shard_map/ppermute | solution.py:32
  3.9 7.2 %collective-permute-start = (bf16[16,144,128]{2,1,0:T(8,128)(2,1)S(1)}, bf16[16,144,128]{2,1,0:T(8,128)(2,1)S(1)}, u32[]{:S(2)}, u32[]{:S(2)}) collective-permute-start(bf16[16,144,128]{2,1,0:T(8,128)(2,1)S(1)} %get-tuple-element.6), channel_id=1, source_target_pairs={{0,1},{1,2},{2,3},{3,4},{4,5},{5,6},{6,7},{7,8},{8,9},{9,10},{10,1... | collective-permute-start | bytes 1769480 | tf_op jit(solution)/shard_map/ppermute | solution.py:30
  11.1 0.6 fusion.6.ram_ref.ram
  11.8 0.9 convert_reduce_fusion.2
  12.7 0.1 convert_reduce_fusion
  12.8 1.4 convert_divide_fusion.band_ref.band
  14.2 0.2 fusion.13
  14.4 0.6 fusion.4.table_ref.table
  15.0 0.7 copy.3.count_ref.count
  15.8 0.5 convert_reduce_fusion.1
  16.3 0.6 fusion.5.sel_ref.sel
  16.9 1.0 collective-permute-done
  18.0 2.9 %constant_dynamic-update-slice_fusion.1 = bf16[160,144,128]{2,1,0:T(8,128)(2,1)S(1)} fusion(bf16[160,144,128]{2,1,0:T(8,128)(2,1)S(1)} %constant_dynamic-update-slice_fusion.2, bf16[128,144,128]{2,1,0:T(8,128)(2,1)} %param.2), kind=kLoop, calls=%fused_computation.26 | loop fusion | bytes 9437184
  20.9 0.0 collective-permute-done.1
  20.9 0.1 constant_dynamic-update-slice_fusion.ext_ref
  21.0 0.0 copy-start
  21.0 2.6 %copy-done = bf16[160,144,128]{2,1,0:T(8,128)(2,1)} copy-done((bf16[160,144,128]{2,1,0:T(8,128)(2,1)}, bf16[160,144,128]{2,1,0:T(8,128)(2,1)S(1)}, u32[]{:S(2)}) %copy-start) | copy-done | bytes 5898264
  23.6 2.4 %slice.12.ext = bf16[160,80,128]{2,1,0:T(8,128)(2,1)} slice(bf16[160,144,128]{2,1,0:T(8,128)(2,1)S(1)} %constant_dynamic-update-slice_fusion.ext_ref), slice={[0:160], [64:144], [0:128]} | slice | bytes 6553600 | tf_op jit(solution)/shard_map/slice | solution.py:265
  25.9 24.8 %shard_map.28.early = bf16[2,64,64,128]{3,2,1,0:T(8,128)(2,1)} custom-call(bf16[160,144,128]{2,1,0:T(8,128)(2,1)} %copy-done, bf16[128,160]{1,0:T(8,128)(2,1)} %fusion.5.sel_ref.sel, f32[128,1]{1,0:T(8,128)} %copy.3.count_ref.count, bf16[128,128]{1,0:T(8,128)(2,1)} %fusion.6.ram_ref.ram, f32[1,128]{1,0:T(1,128)} %bitcast.2, ...), custom_call_target="tpu_custom_call" | custom-call | tf_op jit(solution)/shard_map/pallas_call | solution.py:156
  50.8 120.5 %shard_map.29 = bf16[128,2,2,64,128]{4,3,2,1,0:T(8,128)(2,1)} custom-call(bf16[2,64,64,128]{3,2,1,0:T(8,128)(2,1)} %shard_map.28.early, bf16[160,80,128]{2,1,0:T(8,128)(2,1)} %slice.12.ext, bf16[128,160]{1,0:T(8,128)(2,1)} %fusion.5.sel_ref.sel, f32[128,1]{1,0:T(8,128)} %copy.3.count_ref.count, bf16[128,128]{1,0:T(8,128)(2,1)} %fusion.6.ram_ref.ram, ...), custom_call_target="tpu_custom_call" | custom-call | tf_op jit(solution)/shard_map/pallas_call | solution.py:269
  171.2 10.8 %copy.8 = bf16[128,2,2,64,128]{4,3,2,1,0:T(8,128)(2,1)} copy(bf16[128,2,2,64,128]{4,3,2,1,0:T(8,128)(2,1)} %shard_map.29) | data formatting | bytes 16777216
  (3 shorter events, 0.0 us)
Async XLA Ops:
  1.3 19.6 %collective-permute-start.1 = (bf16[16,144,128]{2,1,0:T(8,128)(2,1)S(1)}, bf16[16,144,128]{2,1,0:T(8,128)(2,1)S(1)}, u32[]{:S(2)}, u32[]{:S(2)}) collective-permute-start(bf16[16,144,128]{2,1,0:T(8,128)(2,1)S(1)} %get-tuple-element.5), channel_id=1, source_target_pairs={{1,0},{2,1},{3,2},{4,3},{5,4},{6,5},{7,6},{8,7},{9,8},{10,9},{11,1... | collective-permute-start | bytes 1769480 | tf_op jit(solution)/shard_map/ppermute | solution.py:32
  3.9 14.0 %collective-permute-start = (bf16[16,144,128]{2,1,0:T(8,128)(2,1)S(1)}, bf16[16,144,128]{2,1,0:T(8,128)(2,1)S(1)}, u32[]{:S(2)}, u32[]{:S(2)}) collective-permute-start(bf16[16,144,128]{2,1,0:T(8,128)(2,1)S(1)} %get-tuple-element.6), channel_id=1, source_target_pairs={{0,1},{1,2},{2,3},{3,4},{4,5},{5,6},{6,7},{7,8},{8,9},{9,10},{10,1... | collective-permute-start | bytes 1769480 | tf_op jit(solution)/shard_map/ppermute | solution.py:30
  21.0 2.6 %copy-start = (bf16[160,144,128]{2,1,0:T(8,128)(2,1)}, bf16[160,144,128]{2,1,0:T(8,128)(2,1)S(1)}, u32[]{:S(2)}) copy-start(bf16[160,144,128]{2,1,0:T(8,128)(2,1)S(1)} %constant_dynamic-update-slice_fusion.ext_ref) | copy-start | bytes 17694724

commit v5 on v4

--- a/solution.py
+++ b/solution.py
@@ -175,8 +175,10 @@
             lhs = x.reshape(-1, x.shape[-1])
             real_rhs = y.reshape(-1, y.shape[-1])
             imag_rhs = jnp.concatenate([-y[1], y[0]], axis=0)
-            real = real + lax.dot_general(lhs, real_rhs, dims, preferred_element_type=jnp.float32)
-            imag = imag + lax.dot_general(lhs, imag_rhs, dims, preferred_element_type=jnp.float32)
+            rhs = jnp.concatenate([real_rhs, imag_rhs], axis=1)
+            both = lax.dot_general(lhs, rhs, dims, preferred_element_type=jnp.float32)
+            real = real + both[:, : y.shape[-1]]
+            imag = imag + both[:, y.shape[-1] :]
         real_rows.append(real / scale)
         imag_rows.append(imag / scale)
     out[:, r, 0, rows, :] = jnp.stack(real_rows, axis=1).astype(out.dtype)

time: 182 us -> 182 us (level)
  the two profiles are of different devices: /device:TPU:249 before, /device:TPU:6 now
where the time goes in v5:
time: 182 us; the launch traced here: 178 us
  Pallas kernels  133 us (73%)
  local copies, waits for them, and re-layouts  20.8 us (11%)
  starting transfers between devices  11.8 us (6%)
  waiting for transfers between devices  7.67 us (4%)
  other arithmetic  5.07 us (3%)
    pallas_call x1, Pallas kernels, per_device(): pl.pallas_call(functools.partial(exchange_kernel, n, chunks, math.sqrt(wi...  108 us
    pallas_call x1, Pallas kernels, prepare_fast(): pl.pallas_call(prepare_kernel, out_shape=jax.ShapeDtypeStruct((2, bin_cou...  24.8 us
    unnamed x5, local copies, waits for them, and re-layouts  16.3 us
    ppermute x1, starting transfers between devices, with_halo(): lax.ppermute(head, axis, [((i + 1) % count, i) for i in range(ends)])  9.92 us
    ppermute x1, waiting for transfers between devices, with_halo(): lax.ppermute(tail, axis, [(i, (i + 1) % count) for i in range(ends)])  7.67 us
  transfers between devices with their start and end apart: 2, of which 1 were waited for; matrix products, arithmetic and copies ran while one was open for 5% of the time, Pallas kernels for 0%

profile of v5, /device:TPU:6, one launch (start us, length us, event | category | flops | bytes accessed | tf_op | source)
XLA Modules:
  0.0 178.4 jit_solution(2055272435370823201)
XLA Ops:
  0.0 1.3 fusion.14
  1.3 9.9 %collective-permute-start.1 = (bf16[16,144,128]{2,1,0:T(8,128)(2,1)S(1)}, bf16[16,144,128]{2,1,0:T(8,128)(2,1)S(1)}, u32[]{:S(2)}, u32[]{:S(2)}) collective-permute-start(bf16[16,144,128]{2,1,0:T(8,128)(2,1)S(1)} %get-tuple-element.5), channel_id=1, source_target_pairs={{1,0},{2,1},{3,2},{4,3},{5,4},{6,5},{7,6},{8,7},{9,8},{10,9},{11,1... | collective-permute-start | bytes 1769480 | tf_op jit(solution)/shard_map/ppermute | solution.py:32
  11.3 1.9 %collective-permute-start = (bf16[16,144,128]{2,1,0:T(8,128)(2,1)S(1)}, bf16[16,144,128]{2,1,0:T(8,128)(2,1)S(1)}, u32[]{:S(2)}, u32[]{:S(2)}) collective-permute-start(bf16[16,144,128]{2,1,0:T(8,128)(2,1)S(1)} %get-tuple-element.6), channel_id=1, source_target_pairs={{0,1},{1,2},{2,3},{3,4},{4,5},{5,6},{6,7},{7,8},{8,9},{9,10},{10,1... | collective-permute-start | bytes 1769480 | tf_op jit(solution)/shard_map/ppermute | solution.py:30
  13.2 0.6 fusion.6.ram_ref.ram
  13.8 0.9 convert_reduce_fusion.2
  14.7 0.1 convert_reduce_fusion
  14.8 1.4 convert_divide_fusion.band_ref.band
  16.3 0.2 fusion.13
  16.5 0.6 fusion.4.table_ref.table
  17.1 0.7 copy.3.count_ref.count
  17.8 0.5 convert_reduce_fusion.1
  18.4 0.6 fusion.5.sel_ref.sel
  19.0 7.7 %collective-permute-done = bf16[16,144,128]{2,1,0:T(8,128)(2,1)S(1)} collective-permute-done((bf16[16,144,128]{2,1,0:T(8,128)(2,1)S(1)}, bf16[16,144,128]{2,1,0:T(8,128)(2,1)S(1)}, u32[]{:S(2)}, u32[]{:S(2)}) %collective-permute-start) | collective-permute-done | bytes 589856 | tf_op jit(solution)/shard_map/ppermute | solution.py:30
  26.7 2.9 %constant_dynamic-update-slice_fusion.1 = bf16[160,144,128]{2,1,0:T(8,128)(2,1)S(1)} fusion(bf16[160,144,128]{2,1,0:T(8,128)(2,1)S(1)} %constant_dynamic-update-slice_fusion.2, bf16[128,144,128]{2,1,0:T(8,128)(2,1)} %param.2), kind=kLoop, calls=%fused_computation.26 | loop fusion | bytes 9437184
  29.7 0.0 collective-permute-done.1
  29.7 0.1 constant_dynamic-update-slice_fusion.ext_ref
  29.8 0.0 copy-start
  29.8 2.6 %copy-done = bf16[160,144,128]{2,1,0:T(8,128)(2,1)} copy-done((bf16[160,144,128]{2,1,0:T(8,128)(2,1)}, bf16[160,144,128]{2,1,0:T(8,128)(2,1)S(1)}, u32[]{:S(2)}) %copy-start) | copy-done | bytes 5898264
  32.3 2.4 %slice.12.ext = bf16[160,80,128]{2,1,0:T(8,128)(2,1)} slice(bf16[160,144,128]{2,1,0:T(8,128)(2,1)S(1)} %constant_dynamic-update-slice_fusion.ext_ref), slice={[0:160], [64:144], [0:128]} | slice | bytes 6553600 | tf_op jit(solution)/shard_map/slice | solution.py:267
  34.7 24.8 %shard_map.28.early = bf16[2,64,64,128]{3,2,1,0:T(8,128)(2,1)} custom-call(bf16[160,144,128]{2,1,0:T(8,128)(2,1)} %copy-done, bf16[128,160]{1,0:T(8,128)(2,1)} %fusion.5.sel_ref.sel, f32[128,1]{1,0:T(8,128)} %copy.3.count_ref.count, bf16[128,128]{1,0:T(8,128)(2,1)} %fusion.6.ram_ref.ram, f32[1,128]{1,0:T(1,128)} %bitcast.2, ...), custom_call_target="tpu_custom_call" | custom-call | tf_op jit(solution)/shard_map/pallas_call | solution.py:156
  59.5 108.1 %shard_map.29 = bf16[128,2,2,64,128]{4,3,2,1,0:T(8,128)(2,1)} custom-call(bf16[2,64,64,128]{3,2,1,0:T(8,128)(2,1)} %shard_map.28.early, bf16[160,80,128]{2,1,0:T(8,128)(2,1)} %slice.12.ext, bf16[128,160]{1,0:T(8,128)(2,1)} %fusion.5.sel_ref.sel, f32[128,1]{1,0:T(8,128)} %copy.3.count_ref.count, bf16[128,128]{1,0:T(8,128)(2,1)} %fusion.6.ram_ref.ram, ...), custom_call_target="tpu_custom_call" | custom-call | tf_op jit(solution)/shard_map/pallas_call | solution.py:271
  167.6 10.8 %copy.8 = bf16[128,2,2,64,128]{4,3,2,1,0:T(8,128)(2,1)} copy(bf16[128,2,2,64,128]{4,3,2,1,0:T(8,128)(2,1)} %shard_map.29) | data formatting | bytes 16777216
  (3 shorter events, 0.0 us)
Async XLA Ops:
  1.3 28.3 %collective-permute-start.1 = (bf16[16,144,128]{2,1,0:T(8,128)(2,1)S(1)}, bf16[16,144,128]{2,1,0:T(8,128)(2,1)S(1)}, u32[]{:S(2)}, u32[]{:S(2)}) collective-permute-start(bf16[16,144,128]{2,1,0:T(8,128)(2,1)S(1)} %get-tuple-element.5), channel_id=1, source_target_pairs={{1,0},{2,1},{3,2},{4,3},{5,4},{6,5},{7,6},{8,7},{9,8},{10,9},{11,1... | collective-permute-start | bytes 1769480 | tf_op jit(solution)/shard_map/ppermute | solution.py:32
  11.3 15.4 %collective-permute-start = (bf16[16,144,128]{2,1,0:T(8,128)(2,1)S(1)}, bf16[16,144,128]{2,1,0:T(8,128)(2,1)S(1)}, u32[]{:S(2)}, u32[]{:S(2)}) collective-permute-start(bf16[16,144,128]{2,1,0:T(8,128)(2,1)S(1)} %get-tuple-element.6), channel_id=1, source_target_pairs={{0,1},{1,2},{2,3},{3,4},{4,5},{5,6},{6,7},{7,8},{8,9},{9,10},{10,1... | collective-permute-start | bytes 1769480 | tf_op jit(solution)/shard_map/ppermute | solution.py:30
  29.8 2.6 %copy-start = (bf16[160,144,128]{2,1,0:T(8,128)(2,1)}, bf16[160,144,128]{2,1,0:T(8,128)(2,1)S(1)}, u32[]{:S(2)}) copy-start(bf16[160,144,128]{2,1,0:T(8,128)(2,1)S(1)} %constant_dynamic-update-slice_fusion.ext_ref) | copy-start | bytes 17694724

commit v6 on v5

--- a/solution.py
+++ b/solution.py
@@ -185,8 +185,8 @@
     out[:, r, 1, rows, :] = jnp.stack(imag_rows, axis=1).astype(out.dtype)
 
 
-def exchange_kernel(n, chunks, scale, step, early, ext, sel, count, ram, ram_count, table, band,
-                    out, late, first, second, first_send, first_recv, second_send, second_recv):
+def exchange_kernel(n, chunks, scale, step, bounds, early, ext, sel, count, ram, ram_count, table, band,
+                    out, lates, first, second, first_send, first_recv, second_send, second_recv):
     me = lax.axis_index("blk")
     core = lax.rem(me, 2)
     down = lax.rem(me + n - 2, n)
@@ -199,7 +199,7 @@
     pl.semaphore_wait(barrier, 3)
 
     size = early.shape[1] // chunks
-    owns = (early, late)
+    owns = [early] + list(lates)
 
     def part(i):
         return pl.ds(pl.multiple_of(i * size, size), size)
@@ -226,19 +226,23 @@
                 to_mate(owns[p], p, i).start()
 
     send_part(0)
-
     consts = [r[...] for r in (sel, count, ram, ram_count, table, band)]
-
-    @pl.loop(0, ext.shape[1] // step)
-    def _(b):
-        windows = pl.ds(pl.multiple_of(b * step, step), step)
-        late[:, :, windows, :] = whiten_block(ext[:, windows, :], *consts).astype(late.dtype)
-
-    send_part(1)
+    for p, (start, length) in enumerate(bounds, start=1):
+        late = lates[p - 1]
+
+        @pl.loop(0, length // step)
+        def _(b):
+            src = pl.ds(pl.multiple_of(start + b * step, step), step)
+            dst = pl.ds(pl.multiple_of(b * step, step), step)
+            late[:, :, dst, :] = whiten_block(ext[:, src, :], *consts).astype(late.dtype)
+
+        send_part(p)
+
+    parts = len(owns)
 
     @pl.loop(0, chunks)
     def _(i):
-        for p in range(2):
+        for p in range(parts):
             to_down(p, i).wait_recv()
 
             @pl.when(core == 0)
@@ -246,46 +250,51 @@
                 to_mate(second[p], p, i).start()
 
         correlate_chunk(owns, second, out, 1, part(i), scale)
-        for p in range(2):
+        for p in range(parts):
             to_mate(second[p], p, i).wait_recv()
         correlate_chunk(owns, first, out, 0, part(i), scale)
 
     @pl.loop(0, chunks)
     def _(i):
-        for p in range(2):
+        for p in range(parts):
             to_down(p, i).wait_send()
             to_mate(second[p], p, i).wait_send()
 
 
-def per_device(traces, bands, chunks=4, early_windows=64):
+def per_device(traces, bands, chunks=4, split=(16, 32, 48, 48), step=16):
     extended = with_halo(traces, (("blk", 0),), HW)
     channel_count, window_count, samples = traces.shape
     n = lax.axis_size("blk")
     first_channel = lax.axis_index("blk") * channel_count
     consts = constants(first_channel, channel_count * n, bands, channel_count, HW, samples, RAM_HALF)
-    early = prepare_fast(extended, consts, early_windows)
-    rest = extended[:, early_windows:]
+    early = prepare_fast(extended, consts, split[0], step)
+    bounds, start = [], split[0]
+    for length in split[1:]:
+        bounds.append((start, length))
+        start += length
     bins = samples // 2
-    late_shape = (2, bins, window_count - early_windows, channel_count)
+    shapes = [(2, bins, length, channel_count) for length in split]
+    buffers = lambda: [pltpu.VMEM(shape, jnp.bfloat16) for shape in shapes]
     vmem = pl.BlockSpec(memory_space=pltpu.VMEM)
+    parts = len(split)
     return pl.pallas_call(
-        functools.partial(exchange_kernel, n, chunks, math.sqrt(window_count), 16),
+        functools.partial(exchange_kernel, n, chunks, math.sqrt(window_count), step, bounds),
         out_shape=jax.ShapeDtypeStruct((channel_count, ROUNDS, 2, bins, channel_count), jnp.bfloat16),
         in_specs=[vmem] * 8,
         out_specs=vmem,
         scratch_shapes=[
-            pltpu.VMEM(late_shape, jnp.bfloat16),
-            [pltpu.VMEM(early.shape, jnp.bfloat16), pltpu.VMEM(late_shape, jnp.bfloat16)],
-            [pltpu.VMEM(early.shape, jnp.bfloat16), pltpu.VMEM(late_shape, jnp.bfloat16)],
-            pltpu.SemaphoreType.DMA((2, chunks)),
-            pltpu.SemaphoreType.DMA((2, chunks)),
-            pltpu.SemaphoreType.DMA((2, chunks)),
-            pltpu.SemaphoreType.DMA((2, chunks)),
+            buffers()[1:],
+            buffers(),
+            buffers(),
+            pltpu.SemaphoreType.DMA((parts, chunks)),
+            pltpu.SemaphoreType.DMA((parts, chunks)),
+            pltpu.SemaphoreType.DMA((parts, chunks)),
+            pltpu.SemaphoreType.DMA((parts, chunks)),
         ],
         compiler_params=pltpu.CompilerParams(
             collective_id=0, has_side_effects=True, vmem_limit_bytes=60 * 1024 * 1024
         ),
-    )(early, rest, *consts)
+    )(early, extended, *consts)
 
 
 def solution(mesh):

time: 182 us -> 164 us (0.901); the launches traced: 178 us -> 163 us
  Pallas kernels: 133 us -> 119 us
    pallas_call x1, Pallas kernels: 24.8 us -> 7.63 us  [prepare_fast(): pl.pallas_call(prepare_kernel, out_shape=jax.ShapeDtypeStruct((2, bin_cou...]
    pallas_call x1, Pallas kernels: 108 us -> 112 us  [per_device(): pl.pallas_call(functools.partial(exchange_kernel, n, chunks, math.sqrt(wi...]
    slice x1 -> x0, local copies, waits for them, and re-layouts: 2.35 us -> none  [per_device(): rest = extended[:, early_windows:]]
    unnamed x5 -> x3, local copies, waits for them, and re-layouts: 16.3 us -> 16.5 us
  transfers between devices with their start and end apart: 2 -> 2, of which waited for: 1 -> 1; matrix products, arithmetic and copies ran while one was open for 5% -> 7% of each run, Pallas kernels for 0% -> 0%
where the time goes in v6:
time: 164 us; the launch traced here: 163 us
  Pallas kernels  119 us (73%)
  local copies, waits for them, and re-layouts  19.4 us (12%)
  starting transfers between devices  11.8 us (7%)
  waiting for transfers between devices  7.68 us (5%)
  other arithmetic  5.06 us (3%)
    pallas_call x1, Pallas kernels, per_device(): pl.pallas_call(functools.partial(exchange_kernel, n, chunks, math.sqrt(wi...  112 us
    unnamed x3, local copies, waits for them, and re-layouts  16.5 us
    ppermute x1, starting transfers between devices, with_halo(): lax.ppermute(head, axis, [((i + 1) % count, i) for i in range(ends)])  9.92 us
    ppermute x1, waiting for transfers between devices, with_halo(): lax.ppermute(tail, axis, [(i, (i + 1) % count) for i in range(ends)])  7.68 us
    pallas_call x1, Pallas kernels, prepare_fast(): pl.pallas_call(prepare_kernel, out_shape=jax.ShapeDtypeStruct((2, bin_cou...  7.63 us
  transfers between devices with their start and end apart: 2, of which 1 were waited for; matrix products, arithmetic and copies ran while one was open for 7% of the time, Pallas kernels for 0%

profile of v6, /device:TPU:6, one launch (start us, length us, event | category | flops | bytes accessed | tf_op | source)
XLA Modules:
  0.0 163.1 jit_solution(895335816588672869)
XLA Ops:
  0.0 1.3 fusion.14
  1.3 9.9 %collective-permute-start.1 = (bf16[16,144,128]{2,1,0:T(8,128)(2,1)S(1)}, bf16[16,144,128]{2,1,0:T(8,128)(2,1)S(1)}, u32[]{:S(2)}, u32[]{:S(2)}) collective-permute-start(bf16[16,144,128]{2,1,0:T(8,128)(2,1)S(1)} %get-tuple-element.5), channel_id=1, source_target_pairs={{1,0},{2,1},{3,2},{4,3},{5,4},{6,5},{7,6},{8,7},{9,8},{10,9},{11,1... | collective-permute-start | bytes 1769480 | tf_op jit(solution)/shard_map/ppermute | solution.py:32
  11.3 1.9 %collective-permute-start = (bf16[16,144,128]{2,1,0:T(8,128)(2,1)S(1)}, bf16[16,144,128]{2,1,0:T(8,128)(2,1)S(1)}, u32[]{:S(2)}, u32[]{:S(2)}) collective-permute-start(bf16[16,144,128]{2,1,0:T(8,128)(2,1)S(1)} %get-tuple-element.6), channel_id=1, source_target_pairs={{0,1},{1,2},{2,3},{3,4},{4,5},{5,6},{6,7},{7,8},{8,9},{9,10},{10,1... | collective-permute-start | bytes 1769480 | tf_op jit(solution)/shard_map/ppermute | solution.py:30
  13.2 0.6 fusion.6.ram_ref.ram
  13.8 0.9 convert_reduce_fusion.2
  14.7 0.1 convert_reduce_fusion
  14.8 1.4 convert_divide_fusion.band_ref.band
  16.3 0.2 fusion.13
  16.5 0.6 fusion.4.table_ref.table
  17.1 0.7 copy.3.count_ref.count
  17.8 0.5 convert_reduce_fusion.1
  18.3 0.6 fusion.5.sel_ref.sel
  19.0 7.7 %collective-permute-done = bf16[16,144,128]{2,1,0:T(8,128)(2,1)S(1)} collective-permute-done((bf16[16,144,128]{2,1,0:T(8,128)(2,1)S(1)}, bf16[16,144,128]{2,1,0:T(8,128)(2,1)S(1)}, u32[]{:S(2)}, u32[]{:S(2)}) %collective-permute-start) | collective-permute-done | bytes 589856 | tf_op jit(solution)/shard_map/ppermute | solution.py:30
  26.7 0.9 constant_dynamic-update-slice_fusion.2
  27.5 4.8 %constant_dynamic-update-slice_fusion.1 = bf16[160,144,128]{2,1,0:T(8,128)(2,1)} fusion(bf16[160,144,128]{2,1,0:T(8,128)(2,1)} %constant_dynamic-update-slice_fusion.2, bf16[128,144,128]{2,1,0:T(8,128)(2,1)} %param.2), kind=kLoop, calls=%fused_computation.26 | loop fusion | bytes 9437184
  32.4 0.0 collective-permute-done.1
  32.4 0.9 constant_dynamic-update-slice_fusion.ext_ref.ext
  33.2 7.6 %shard_map.28.early = bf16[2,64,16,128]{3,2,1,0:T(8,128)(2,1)} custom-call(bf16[160,144,128]{2,1,0:T(8,128)(2,1)} %constant_dynamic-update-slice_fusion.ext_ref.ext, bf16[128,160]{1,0:T(8,128)(2,1)} %fusion.5.sel_ref.sel, f32[128,1]{1,0:T(8,128)} %copy.3.count_ref.count, bf16[128,128]{1,0:T(8,128)(2,1)} %fusion.6.ram_ref.ram, f32[1,128]{1,0:T(1,128)} %bitcast.2, ...), custom_call_target="tpu_custom_call" | custom-call | tf_op jit(solution)/shard_map/pallas_call | solution.py:156
  40.8 111.5 %shard_map.29 = bf16[128,2,2,64,128]{4,3,2,1,0:T(8,128)(2,1)} custom-call(bf16[2,64,16,128]{3,2,1,0:T(8,128)(2,1)} %shard_map.28.early, bf16[160,144,128]{2,1,0:T(8,128)(2,1)} %constant_dynamic-update-slice_fusion.ext_ref.ext, bf16[128,160]{1,0:T(8,128)(2,1)} %fusion.5.sel_ref.sel, f32[128,1]{1,0:T(8,128)} %copy.3.count_ref.count, ...), custom_call_target="tpu_custom_call" | custom-call | tf_op jit(solution)/shard_map/pallas_call | solution.py:280
  152.4 10.8 %copy.8 = bf16[128,2,2,64,128]{4,3,2,1,0:T(8,128)(2,1)} copy(bf16[128,2,2,64,128]{4,3,2,1,0:T(8,128)(2,1)} %shard_map.29) | data formatting | bytes 16777216
  (2 shorter events, 0.0 us)
Async XLA Ops:
  1.3 31.0 %collective-permute-start.1 = (bf16[16,144,128]{2,1,0:T(8,128)(2,1)S(1)}, bf16[16,144,128]{2,1,0:T(8,128)(2,1)S(1)}, u32[]{:S(2)}, u32[]{:S(2)}) collective-permute-start(bf16[16,144,128]{2,1,0:T(8,128)(2,1)S(1)} %get-tuple-element.5), channel_id=1, source_target_pairs={{1,0},{2,1},{3,2},{4,3},{5,4},{6,5},{7,6},{8,7},{9,8},{10,9},{11,1... | collective-permute-start | bytes 1769480 | tf_op jit(solution)/shard_map/ppermute | solution.py:32
  11.3 15.4 %collective-permute-start = (bf16[16,144,128]{2,1,0:T(8,128)(2,1)S(1)}, bf16[16,144,128]{2,1,0:T(8,128)(2,1)S(1)}, u32[]{:S(2)}, u32[]{:S(2)}) collective-permute-start(bf16[16,144,128]{2,1,0:T(8,128)(2,1)S(1)} %get-tuple-element.6), channel_id=1, source_target_pairs={{0,1},{1,2},{2,3},{3,4},{4,5},{5,6},{6,7},{7,8},{8,9},{9,10},{10,1... | collective-permute-start | bytes 1769480 | tf_op jit(solution)/shard_map/ppermute | solution.py:30

commit v7 on v6

--- a/solution.py
+++ b/solution.py
@@ -163,30 +163,34 @@
     )(extended, *consts)
 
 
-def correlate_chunk(owns, partners, out, r, rows, scale):
+def correlate_chunk(own, partner, acc, out, r, rows, scale, mode):
     dims = (((0,), (0,)), ((), ()))
+    width = own.shape[-1]
     real_rows, imag_rows = [], []
     for j in range(rows.size):
         f = rows.start + j
-        real, imag = 0.0, 0.0
-        for own, partner in zip(owns, partners):
-            x = own[:, f]
-            y = partner[:, f]
-            lhs = x.reshape(-1, x.shape[-1])
-            real_rhs = y.reshape(-1, y.shape[-1])
-            imag_rhs = jnp.concatenate([-y[1], y[0]], axis=0)
-            rhs = jnp.concatenate([real_rhs, imag_rhs], axis=1)
-            both = lax.dot_general(lhs, rhs, dims, preferred_element_type=jnp.float32)
-            real = real + both[:, : y.shape[-1]]
-            imag = imag + both[:, y.shape[-1] :]
-        real_rows.append(real / scale)
-        imag_rows.append(imag / scale)
-    out[:, r, 0, rows, :] = jnp.stack(real_rows, axis=1).astype(out.dtype)
-    out[:, r, 1, rows, :] = jnp.stack(imag_rows, axis=1).astype(out.dtype)
+        x = own[:, f]
+        y = partner[:, f]
+        lhs = x.reshape(-1, x.shape[-1])
+        real_rhs = y.reshape(-1, y.shape[-1])
+        imag_rhs = jnp.concatenate([-y[1], y[0]], axis=0)
+        rhs = jnp.concatenate([real_rhs, imag_rhs], axis=1)
+        both = lax.dot_general(lhs, rhs, dims, preferred_element_type=jnp.float32)
+        if mode == "first":
+            acc[r, f] = both
+        elif mode == "middle":
+            acc[r, f] = acc[r, f] + both
+        else:
+            total = acc[r, f] + both
+            real_rows.append(total[:, :width] / scale)
+            imag_rows.append(total[:, width:] / scale)
+    if mode == "last":
+        out[:, r, 0, rows, :] = jnp.stack(real_rows, axis=1).astype(out.dtype)
+        out[:, r, 1, rows, :] = jnp.stack(imag_rows, axis=1).astype(out.dtype)
 
 
 def exchange_kernel(n, chunks, scale, step, bounds, early, ext, sel, count, ram, ram_count, table, band,
-                    out, lates, first, second, first_send, first_recv, second_send, second_recv):
+                    out, lates, first, second, acc, first_send, first_recv, second_send, second_recv):
     me = lax.axis_index("blk")
     core = lax.rem(me, 2)
     down = lax.rem(me + n - 2, n)
@@ -239,20 +243,20 @@
         send_part(p)
 
     parts = len(owns)
-
-    @pl.loop(0, chunks)
-    def _(i):
-        for p in range(parts):
+    for p in range(parts):
+        mode = "first" if p == 0 else ("last" if p == parts - 1 else "middle")
+
+        @pl.loop(0, chunks)
+        def _(i):
             to_down(p, i).wait_recv()
 
             @pl.when(core == 0)
             def _():
                 to_mate(second[p], p, i).start()
 
-        correlate_chunk(owns, second, out, 1, part(i), scale)
-        for p in range(parts):
+            correlate_chunk(owns[p], second[p], acc, out, 1, part(i), scale, mode)
             to_mate(second[p], p, i).wait_recv()
-        correlate_chunk(owns, first, out, 0, part(i), scale)
+            correlate_chunk(owns[p], first[p], acc, out, 0, part(i), scale, mode)
 
     @pl.loop(0, chunks)
     def _(i):
@@ -286,13 +290,14 @@
             buffers()[1:],
             buffers(),
             buffers(),
+            pltpu.VMEM((ROUNDS, bins, channel_count, 2 * channel_count), jnp.float32),
             pltpu.SemaphoreType.DMA((parts, chunks)),
             pltpu.SemaphoreType.DMA((parts, chunks)),
             pltpu.SemaphoreType.DMA((parts, chunks)),
             pltpu.SemaphoreType.DMA((parts, chunks)),
         ],
         compiler_params=pltpu.CompilerParams(
-            collective_id=0, has_side_effects=True, vmem_limit_bytes=60 * 1024 * 1024
+            collective_id=0, has_side_effects=True, vmem_limit_bytes=63 * 1024 * 1024
         ),
     )(early, extended, *consts)
 

time: 164 us -> 164 us (level); the launches traced: 163 us -> 161 us
  Pallas kernels: 119 us -> 117 us
    pallas_call x1, Pallas kernels: 112 us -> 110 us  [per_device(): pl.pallas_call(functools.partial(exchange_kernel, n, chunks, math.sqrt(wi...]
where the time goes in v7:
time: 164 us; the launch traced here: 161 us
  Pallas kernels  117 us (71%)
  local copies, waits for them, and re-layouts  19.4 us (12%)
  starting transfers between devices  11.8 us (7%)
  waiting for transfers between devices  7.68 us (5%)
  other arithmetic  5.06 us (3%)
    pallas_call x1, Pallas kernels, per_device(): pl.pallas_call(functools.partial(exchange_kernel, n, chunks, math.sqrt(wi...  110 us
    unnamed x3, local copies, waits for them, and re-layouts  16.5 us
    ppermute x1, starting transfers between devices, with_halo(): lax.ppermute(head, axis, [((i + 1) % count, i) for i in range(ends)])  9.92 us
    ppermute x1, waiting for transfers between devices, with_halo(): lax.ppermute(tail, axis, [(i, (i + 1) % count) for i in range(ends)])  7.68 us
    pallas_call x1, Pallas kernels, prepare_fast(): pl.pallas_call(prepare_kernel, out_shape=jax.ShapeDtypeStruct((2, bin_cou...  7.63 us
  transfers between devices with their start and end apart: 2, of which 1 were waited for; matrix products, arithmetic and copies ran while one was open for 7% of the time, Pallas kernels for 0%

profile of v7, /device:TPU:6, one launch (start us, length us, event | category | flops | bytes accessed | tf_op | source)
XLA Modules:
  0.0 161.3 jit_solution(2150704238770889062)
XLA Ops:
  0.0 1.3 fusion.14
  1.3 9.9 %collective-permute-start.1 = (bf16[16,144,128]{2,1,0:T(8,128)(2,1)S(1)}, bf16[16,144,128]{2,1,0:T(8,128)(2,1)S(1)}, u32[]{:S(2)}, u32[]{:S(2)}) collective-permute-start(bf16[16,144,128]{2,1,0:T(8,128)(2,1)S(1)} %get-tuple-element.5), channel_id=1, source_target_pairs={{1,0},{2,1},{3,2},{4,3},{5,4},{6,5},{7,6},{8,7},{9,8},{10,9},{11,1... | collective-permute-start | bytes 1769480 | tf_op jit(solution)/shard_map/ppermute | solution.py:32
  11.3 1.9 %collective-permute-start = (bf16[16,144,128]{2,1,0:T(8,128)(2,1)S(1)}, bf16[16,144,128]{2,1,0:T(8,128)(2,1)S(1)}, u32[]{:S(2)}, u32[]{:S(2)}) collective-permute-start(bf16[16,144,128]{2,1,0:T(8,128)(2,1)S(1)} %get-tuple-element.6), channel_id=1, source_target_pairs={{0,1},{1,2},{2,3},{3,4},{4,5},{5,6},{6,7},{7,8},{8,9},{9,10},{10,1... | collective-permute-start | bytes 1769480 | tf_op jit(solution)/shard_map/ppermute | solution.py:30
  13.2 0.6 fusion.6.ram_ref.ram
  13.8 0.9 convert_reduce_fusion.2
  14.7 0.1 convert_reduce_fusion
  14.8 1.4 convert_divide_fusion.band_ref.band
  16.3 0.2 fusion.13
  16.5 0.6 fusion.4.table_ref.table
  17.1 0.7 copy.3.count_ref.count
  17.8 0.5 convert_reduce_fusion.1
  18.3 0.6 fusion.5.sel_ref.sel
  19.0 7.7 %collective-permute-done = bf16[16,144,128]{2,1,0:T(8,128)(2,1)S(1)} collective-permute-done((bf16[16,144,128]{2,1,0:T(8,128)(2,1)S(1)}, bf16[16,144,128]{2,1,0:T(8,128)(2,1)S(1)}, u32[]{:S(2)}, u32[]{:S(2)}) %collective-permute-start) | collective-permute-done | bytes 589856 | tf_op jit(solution)/shard_map/ppermute | solution.py:30
  26.7 0.9 constant_dynamic-update-slice_fusion.2
  27.5 4.8 %constant_dynamic-update-slice_fusion.1 = bf16[160,144,128]{2,1,0:T(8,128)(2,1)} fusion(bf16[160,144,128]{2,1,0:T(8,128)(2,1)} %constant_dynamic-update-slice_fusion.2, bf16[128,144,128]{2,1,0:T(8,128)(2,1)} %param.2), kind=kLoop, calls=%fused_computation.26 | loop fusion | bytes 9437184
  32.4 0.0 collective-permute-done.1
  32.4 0.9 constant_dynamic-update-slice_fusion.ext_ref.ext
  33.2 7.6 %shard_map.28.early = bf16[2,64,16,128]{3,2,1,0:T(8,128)(2,1)} custom-call(bf16[160,144,128]{2,1,0:T(8,128)(2,1)} %constant_dynamic-update-slice_fusion.ext_ref.ext, bf16[128,160]{1,0:T(8,128)(2,1)} %fusion.5.sel_ref.sel, f32[128,1]{1,0:T(8,128)} %copy.3.count_ref.count, bf16[128,128]{1,0:T(8,128)(2,1)} %fusion.6.ram_ref.ram, f32[1,128]{1,0:T(1,128)} %bitcast.2, ...), custom_call_target="tpu_custom_call" | custom-call | tf_op jit(solution)/shard_map/pallas_call | solution.py:156
  40.8 109.7 %shard_map.29 = bf16[128,2,2,64,128]{4,3,2,1,0:T(8,128)(2,1)} custom-call(bf16[2,64,16,128]{3,2,1,0:T(8,128)(2,1)} %shard_map.28.early, bf16[160,144,128]{2,1,0:T(8,128)(2,1)} %constant_dynamic-update-slice_fusion.ext_ref.ext, bf16[128,160]{1,0:T(8,128)(2,1)} %fusion.5.sel_ref.sel, f32[128,1]{1,0:T(8,128)} %copy.3.count_ref.count, ...), custom_call_target="tpu_custom_call" | custom-call | tf_op jit(solution)/shard_map/pallas_call | solution.py:284
  150.5 10.8 %copy.8 = bf16[128,2,2,64,128]{4,3,2,1,0:T(8,128)(2,1)} copy(bf16[128,2,2,64,128]{4,3,2,1,0:T(8,128)(2,1)} %shard_map.29) | data formatting | bytes 16777216
  (2 shorter events, 0.0 us)
Async XLA Ops:
  1.3 31.0 %collective-permute-start.1 = (bf16[16,144,128]{2,1,0:T(8,128)(2,1)S(1)}, bf16[16,144,128]{2,1,0:T(8,128)(2,1)S(1)}, u32[]{:S(2)}, u32[]{:S(2)}) collective-permute-start(bf16[16,144,128]{2,1,0:T(8,128)(2,1)S(1)} %get-tuple-element.5), channel_id=1, source_target_pairs={{1,0},{2,1},{3,2},{4,3},{5,4},{6,5},{7,6},{8,7},{9,8},{10,9},{11,1... | collective-permute-start | bytes 1769480 | tf_op jit(solution)/shard_map/ppermute | solution.py:32
  11.3 15.4 %collective-permute-start = (bf16[16,144,128]{2,1,0:T(8,128)(2,1)S(1)}, bf16[16,144,128]{2,1,0:T(8,128)(2,1)S(1)}, u32[]{:S(2)}, u32[]{:S(2)}) collective-permute-start(bf16[16,144,128]{2,1,0:T(8,128)(2,1)S(1)} %get-tuple-element.6), channel_id=1, source_target_pairs={{0,1},{1,2},{2,3},{3,4},{4,5},{5,6},{6,7},{7,8},{8,9},{9,10},{10,1... | collective-permute-start | bytes 1769480 | tf_op jit(solution)/shard_map/ppermute | solution.py:30

commit v8 on v7

--- a/solution.py
+++ b/solution.py
@@ -189,21 +189,34 @@
         out[:, r, 1, rows, :] = jnp.stack(imag_rows, axis=1).astype(out.dtype)
 
 
-def exchange_kernel(n, chunks, scale, step, bounds, early, ext, sel, count, ram, ram_count, table, band,
-                    out, lates, first, second, acc, first_send, first_recv, second_send, second_recv):
+def exchange_kernel(n, chunks, scale, step, bounds, traces, sel, count, ram, ram_count, table, band,
+                    out, head, tail, owns, first, second, acc, halo_send, halo_recv,
+                    first_send, first_recv, second_send, second_recv):
     me = lax.axis_index("blk")
     core = lax.rem(me, 2)
     down = lax.rem(me + n - 2, n)
     up = lax.rem(me + 2, n)
+    left = lax.rem(me + n - 1, n)
+    right = lax.rem(me + 1, n)
     mate = me + 1 - 2 * core
+    halo = head.shape[0]
+    channels = traces.shape[0]
 
     barrier = pltpu.get_barrier_semaphore()
-    for peer in (down, up, mate):
+    for peer in (down, up, left, right):
         pl.semaphore_signal(barrier, inc=1, device_id=(peer,), device_id_type=MESH)
-    pl.semaphore_wait(barrier, 3)
-
-    size = early.shape[1] // chunks
-    owns = [early] + list(lates)
+    pl.semaphore_wait(barrier, 4)
+
+    to_right = pltpu.make_async_remote_copy(
+        traces.at[pl.ds(channels - halo, halo)], head, halo_send.at[0], halo_recv.at[0],
+        device_id=(right,), device_id_type=MESH)
+    to_left = pltpu.make_async_remote_copy(
+        traces.at[pl.ds(0, halo)], tail, halo_send.at[1], halo_recv.at[1],
+        device_id=(left,), device_id_type=MESH)
+    to_right.start()
+    to_left.start()
+
+    size = owns[0].shape[1] // chunks
 
     def part(i):
         return pl.ds(pl.multiple_of(i * size, size), size)
@@ -229,16 +242,18 @@
             def _(i):
                 to_mate(owns[p], p, i).start()
 
-    send_part(0)
     consts = [r[...] for r in (sel, count, ram, ram_count, table, band)]
-    for p, (start, length) in enumerate(bounds, start=1):
-        late = lates[p - 1]
+    to_right.wait_recv()
+    to_left.wait_recv()
+    for p, (start, length) in enumerate(bounds):
+        late = owns[p]
 
         @pl.loop(0, length // step)
         def _(b):
             src = pl.ds(pl.multiple_of(start + b * step, step), step)
             dst = pl.ds(pl.multiple_of(b * step, step), step)
-            late[:, :, dst, :] = whiten_block(ext[:, src, :], *consts).astype(late.dtype)
+            block = jnp.concatenate([head[:, src, :], traces[:, src, :], tail[:, src, :]], axis=0)
+            late[:, :, dst, :] = whiten_block(block, *consts).astype(late.dtype)
 
         send_part(p)
 
@@ -257,6 +272,9 @@
             correlate_chunk(owns[p], second[p], acc, out, 1, part(i), scale, mode)
             to_mate(second[p], p, i).wait_recv()
             correlate_chunk(owns[p], first[p], acc, out, 0, part(i), scale, mode)
+
+    to_right.wait_send()
+    to_left.wait_send()
 
     @pl.loop(0, chunks)
     def _(i):
@@ -266,14 +284,12 @@
 
 
 def per_device(traces, bands, chunks=4, split=(16, 32, 48, 48), step=16):
-    extended = with_halo(traces, (("blk", 0),), HW)
     channel_count, window_count, samples = traces.shape
     n = lax.axis_size("blk")
     first_channel = lax.axis_index("blk") * channel_count
     consts = constants(first_channel, channel_count * n, bands, channel_count, HW, samples, RAM_HALF)
-    early = prepare_fast(extended, consts, split[0], step)
-    bounds, start = [], split[0]
-    for length in split[1:]:
+    bounds, start = [], 0
+    for length in split:
         bounds.append((start, length))
         start += length
     bins = samples // 2
@@ -284,13 +300,17 @@
     return pl.pallas_call(
         functools.partial(exchange_kernel, n, chunks, math.sqrt(window_count), step, bounds),
         out_shape=jax.ShapeDtypeStruct((channel_count, ROUNDS, 2, bins, channel_count), jnp.bfloat16),
-        in_specs=[vmem] * 8,
+        in_specs=[vmem] * 7,
         out_specs=vmem,
         scratch_shapes=[
-            buffers()[1:],
+            pltpu.VMEM((HW, window_count, samples), jnp.bfloat16),
+            pltpu.VMEM((HW, window_count, samples), jnp.bfloat16),
+            buffers(),
             buffers(),
             buffers(),
             pltpu.VMEM((ROUNDS, bins, channel_count, 2 * channel_count), jnp.float32),
+            pltpu.SemaphoreType.DMA((2,)),
+            pltpu.SemaphoreType.DMA((2,)),
             pltpu.SemaphoreType.DMA((parts, chunks)),
             pltpu.SemaphoreType.DMA((parts, chunks)),
             pltpu.SemaphoreType.DMA((parts, chunks)),
@@ -299,7 +319,7 @@
         compiler_params=pltpu.CompilerParams(
             collective_id=0, has_side_effects=True, vmem_limit_bytes=63 * 1024 * 1024
         ),
-    )(early, extended, *consts)
+    )(traces, *consts)
 
 
 def solution(mesh):

time: 164 us -> 151 us (0.921)
  Pallas kernels: 117 us -> 132 us
  starting transfers between devices: 11.8 us -> 0 us
  local copies, waits for them, and re-layouts: 19.4 us -> 11.5 us
  waiting for transfers between devices: 7.68 us -> 0 us
    pallas_call x1, Pallas kernels: 110 us -> 132 us  [per_device(): pl.pallas_call(functools.partial(exchange_kernel, n, chunks, math.sqrt(wi...]
    ppermute x2 -> x0, starting transfers between devices: 11.8 us -> none  [the longest x1 9.92 us: with_halo(): lax.ppermute(head, axis, [((i + 1) % count, i) for i in range(ends)])]
    ppermute x2 -> x0, waiting for transfers between devices: 7.68 us -> none  [the longest x1 7.68 us: with_halo(): lax.ppermute(tail, axis, [(i, (i + 1) % count) for i in range(ends)])]
    pallas_call x1 -> x0, Pallas kernels: 7.63 us -> none  [prepare_fast(): pl.pallas_call(prepare_kernel, out_shape=jax.ShapeDtypeStruct((2, bin_cou...]
    unnamed x3 -> x1, local copies, waits for them, and re-layouts: 16.5 us -> 10.8 us
  transfers between devices with their start and end apart: 2 -> 0, of which waited for: 1 -> 0; matrix products, arithmetic and copies ran while one was open for 7% -> 0% of each run, Pallas kernels for 0% -> 0%
where the time goes in v8:
time: 151 us; the launch traced here: 148 us
  Pallas kernels  132 us (87%)
  local copies, waits for them, and re-layouts  11.5 us (8%)
  other arithmetic  5.16 us (3%)
    pallas_call x1, Pallas kernels, per_device(): pl.pallas_call(functools.partial(exchange_kernel, n, chunks, math.sqrt(wi...  132 us
    unnamed x1, local copies, waits for them, and re-layouts  10.8 us

profile of v8, /device:TPU:6, one launch (start us, length us, event | category | flops | bytes accessed | tf_op | source)
XLA Modules:
  0.0 148.3 jit_solution(1377339974285120988)
XLA Ops:
  0.0 0.9 convert_reduce_fusion.2
  0.9 0.1 convert_reduce_fusion
  1.1 0.6 convert_reduce_fusion.1
  1.7 1.4 convert_divide_fusion.band
  3.1 0.6 fusion.6.ram
  3.7 0.7 copy.3.count
  4.4 0.7 fusion.5.sel
  5.1 0.2 fusion.13
  5.3 0.6 fusion.4.table
  5.9 131.6 %shard_map.28 = bf16[128,2,2,64,128]{4,3,2,1,0:T(8,128)(2,1)} custom-call(bf16[128,144,128]{2,1,0:T(8,128)(2,1)} %traces.1, bf16[128,160]{1,0:T(8,128)(2,1)} %fusion.5.sel, f32[128,1]{1,0:T(8,128)} %copy.3.count, bf16[128,128]{1,0:T(8,128)(2,1)} %fusion.6.ram, f32[1,128]{1,0:T(1,128)} %bitcast.3, bf16[128,128]{1,0:T(8,128)(2,1)} %fusion.4.table, ...), custom_call_target="tpu_custom_call" | custom-call | tf_op jit(solution)/shard_map/pallas_call | solution.py:300
  137.6 10.8 %copy.5 = bf16[128,2,2,64,128]{4,3,2,1,0:T(8,128)(2,1)} copy(bf16[128,2,2,64,128]{4,3,2,1,0:T(8,128)(2,1)} %shard_map.28) | data formatting | bytes 16777216
  (2 shorter events, 0.0 us)

commit v9 on v8

--- a/solution.py
+++ b/solution.py
@@ -163,30 +163,34 @@
     )(extended, *consts)
 
 
-def correlate_chunk(own, partner, acc, out, r, rows, scale, mode):
+def correlate_chunk(own, partners, acc, out, rows, scale, mode):
     dims = (((0,), (0,)), ((), ()))
     width = own.shape[-1]
-    real_rows, imag_rows = [], []
+    pieces = [[[] for _ in range(2)] for _ in partners]
     for j in range(rows.size):
         f = rows.start + j
         x = own[:, f]
-        y = partner[:, f]
-        lhs = x.reshape(-1, x.shape[-1])
-        real_rhs = y.reshape(-1, y.shape[-1])
-        imag_rhs = jnp.concatenate([-y[1], y[0]], axis=0)
-        rhs = jnp.concatenate([real_rhs, imag_rhs], axis=1)
+        lhs = x.reshape(-1, width)
+        sides = []
+        for partner in partners:
+            y = partner[:, f]
+            sides += [y.reshape(-1, width), jnp.concatenate([-y[1], y[0]], axis=0)]
+        rhs = jnp.concatenate(sides, axis=1)
         both = lax.dot_general(lhs, rhs, dims, preferred_element_type=jnp.float32)
         if mode == "first":
-            acc[r, f] = both
+            acc[f] = both
         elif mode == "middle":
-            acc[r, f] = acc[r, f] + both
+            acc[f] = acc[f] + both
         else:
-            total = acc[r, f] + both
-            real_rows.append(total[:, :width] / scale)
-            imag_rows.append(total[:, width:] / scale)
+            total = acc[f] + both
+            for r in range(len(partners)):
+                for o in range(2):
+                    k = 2 * r + o
+                    pieces[r][o].append(total[:, k * width : (k + 1) * width] / scale)
     if mode == "last":
-        out[:, r, 0, rows, :] = jnp.stack(real_rows, axis=1).astype(out.dtype)
-        out[:, r, 1, rows, :] = jnp.stack(imag_rows, axis=1).astype(out.dtype)
+        for r in range(len(partners)):
+            for o in range(2):
+                out[:, r, o, rows, :] = jnp.stack(pieces[r][o], axis=1).astype(out.dtype)
 
 
 def exchange_kernel(n, chunks, scale, step, bounds, traces, sel, count, ram, ram_count, table, band,
@@ -269,9 +273,8 @@
             def _():
                 to_mate(second[p], p, i).start()
 
-            correlate_chunk(owns[p], second[p], acc, out, 1, part(i), scale, mode)
             to_mate(second[p], p, i).wait_recv()
-            correlate_chunk(owns[p], first[p], acc, out, 0, part(i), scale, mode)
+            correlate_chunk(owns[p], (first[p], second[p]), acc, out, part(i), scale, mode)
 
     to_right.wait_send()
     to_left.wait_send()
@@ -308,7 +311,7 @@
             buffers(),
             buffers(),
             buffers(),
-            pltpu.VMEM((ROUNDS, bins, channel_count, 2 * channel_count), jnp.float32),
+            pltpu.VMEM((bins, channel_count, 2 * ROUNDS * channel_count), jnp.float32),
             pltpu.SemaphoreType.DMA((2,)),
             pltpu.SemaphoreType.DMA((2,)),
             pltpu.SemaphoreType.DMA((parts, chunks)),

time: 151 us -> 153 us (1.013)
  the two profiles are of different devices: /device:TPU:6 before, /device:TPU:1 now
where the time goes in v9:
time: 153 us
  Pallas kernels  136 us (89%)
  local copies, waits for them, and re-layouts  11.5 us (8%)
  other arithmetic  5.16 us (3%)
    pallas_call x1, Pallas kernels, per_device(): pl.pallas_call(functools.partial(exchange_kernel, n, chunks, math.sqrt(wi...  136 us
    unnamed x1, local copies, waits for them, and re-layouts  10.8 us

profile of v9, /device:TPU:1, one launch (start us, length us, event | category | flops | bytes accessed | tf_op | source)
XLA Modules:
  0.0 152.7 jit_solution(11697562325193509770)
XLA Ops:
  0.0 0.9 convert_reduce_fusion.2
  0.9 0.1 convert_reduce_fusion
  1.1 0.6 convert_reduce_fusion.1
  1.7 1.4 convert_divide_fusion.band
  3.1 0.6 fusion.6.ram
  3.7 0.7 copy.3.count
  4.4 0.7 fusion.5.sel
  5.1 0.2 fusion.13
  5.3 0.6 fusion.4.table
  5.9 136.0 %shard_map.28 = bf16[128,2,2,64,128]{4,3,2,1,0:T(8,128)(2,1)} custom-call(bf16[128,144,128]{2,1,0:T(8,128)(2,1)} %traces.1, bf16[128,160]{1,0:T(8,128)(2,1)} %fusion.5.sel, f32[128,1]{1,0:T(8,128)} %copy.3.count, bf16[128,128]{1,0:T(8,128)(2,1)} %fusion.6.ram, f32[1,128]{1,0:T(1,128)} %bitcast.3, bf16[128,128]{1,0:T(8,128)(2,1)} %fusion.4.table, ...), custom_call_target="tpu_custom_call" | custom-call | tf_op jit(solution)/shard_map/pallas_call | solution.py:303
  141.9 10.8 %copy.5 = bf16[128,2,2,64,128]{4,3,2,1,0:T(8,128)(2,1)} copy(bf16[128,2,2,64,128]{4,3,2,1,0:T(8,128)(2,1)} %shard_map.28) | data formatting | bytes 16777216
  (2 shorter events, 0.0 us)

commit v10 on v9

--- a/solution.py
+++ b/solution.py
@@ -96,9 +96,9 @@
     for w in range(block.shape[0]):
         x = block[w]
         neighbour_sum = jnp.dot(sel, x.astype(jnp.bfloat16), preferred_element_type=jnp.float32)
-        balanced = (x[halo : halo + channels] - neighbour_sum / count).astype(jnp.bfloat16)
+        balanced = (x[halo : halo + channels] - neighbour_sum * count).astype(jnp.bfloat16)
         ram_sum = jnp.dot(jnp.abs(balanced), ram, preferred_element_type=jnp.float32)
-        envelope = ram_sum / ram_count + epsilon
+        envelope = ram_sum * ram_count + epsilon
         normalized = (balanced.astype(jnp.float32) / envelope).astype(jnp.bfloat16)
         spectra = lax.dot_general(
             table, normalized, (((1,), (1,)), ((), ())), preferred_element_type=jnp.float32
@@ -140,9 +140,9 @@
     band_matrix = same_band / jnp.sum(same_band, axis=1, keepdims=True)
     return [
         selector.astype(jnp.bfloat16),
-        neighbour_count,
+        1.0 / neighbour_count,
         ram_band.astype(jnp.bfloat16),
-        ram_count,
+        1.0 / ram_count,
         dft_table,
         band_matrix,
     ]

time: 153 us -> 153 us (level)
  no operation moved by 1% of the time
where the time goes in v10:
time: 153 us
  Pallas kernels  136 us (89%)
  local copies, waits for them, and re-layouts  11.5 us (8%)
  other arithmetic  5.18 us (3%)
    pallas_call x1, Pallas kernels, per_device(): pl.pallas_call(functools.partial(exchange_kernel, n, chunks, math.sqrt(wi...  136 us
    unnamed x1, local copies, waits for them, and re-layouts  10.8 us

profile of v10, /device:TPU:1, one launch (start us, length us, event | category | flops | bytes accessed | tf_op | source)
XLA Modules:
  0.0 152.7 jit_solution(12838525298674705394)
XLA Ops:
  0.0 0.9 convert_reduce_fusion.2
  0.9 0.1 convert_reduce_fusion
  1.1 0.6 divide_bitcast_fusion.ram_count
  1.7 1.4 convert_divide_fusion.band
  3.1 0.6 fusion.6.ram
  3.7 0.7 copy.3.count
  4.5 0.7 fusion.5.sel
  5.1 0.2 fusion.13
  5.4 0.6 fusion.4.table
  6.0 136.0 %shard_map.28 = bf16[128,2,2,64,128]{4,3,2,1,0:T(8,128)(2,1)} custom-call(bf16[128,144,128]{2,1,0:T(8,128)(2,1)} %traces.1, bf16[128,160]{1,0:T(8,128)(2,1)} %fusion.5.sel, f32[128,1]{1,0:T(8,128)} %copy.3.count, bf16[128,128]{1,0:T(8,128)(2,1)} %fusion.6.ram, f32[1,128]{1,0:T(1,128)} %divide_bitcast_fusion.ram_count, bf16[128,128]{1,0:T(8,128)(2,1)} %fusion.4.table, ...), custom_call_target="tpu_custom_call" | custom-call | tf_op jit(solution)/shard_map/pallas_call | solution.py:303
  142.0 10.8 %copy.5 = bf16[128,2,2,64,128]{4,3,2,1,0:T(8,128)(2,1)} copy(bf16[128,2,2,64,128]{4,3,2,1,0:T(8,128)(2,1)} %shard_map.28) | data formatting | bytes 16777216
  (4 shorter events, 0.1 us)

commit v11 on v8

--- a/solution.py
+++ b/solution.py
@@ -283,7 +283,7 @@
             to_mate(second[p], p, i).wait_send()
 
 
-def per_device(traces, bands, chunks=4, split=(16, 32, 48, 48), step=16):
+def per_device(traces, bands, chunks=2, split=(16, 32, 48, 48), step=16):
     channel_count, window_count, samples = traces.shape
     n = lax.axis_size("blk")
     first_channel = lax.axis_index("blk") * channel_count

time: 151 us -> 154 us (1.020)
  Pallas kernels: 132 us -> 135 us
    pallas_call x1, Pallas kernels: 132 us -> 135 us  [per_device(): pl.pallas_call(functools.partial(exchange_kernel, n, chunks, math.sqrt(wi...]
where the time goes in v11:
time: 154 us; the launch traced here: 152 us
  Pallas kernels  135 us (88%)
  local copies, waits for them, and re-layouts  11.5 us (7%)
  other arithmetic  5.16 us (3%)
    pallas_call x1, Pallas kernels, per_device(): pl.pallas_call(functools.partial(exchange_kernel, n, chunks, math.sqrt(wi...  135 us
    unnamed x1, local copies, waits for them, and re-layouts  10.8 us

profile of v11, /device:TPU:6, one launch (start us, length us, event | category | flops | bytes accessed | tf_op | source)
XLA Modules:
  0.0 151.9 jit_solution(16293327469172113130)
XLA Ops:
  0.0 0.9 convert_reduce_fusion.2
  0.9 0.1 convert_reduce_fusion
  1.1 0.6 convert_reduce_fusion.1
  1.7 1.4 convert_divide_fusion.band
  3.1 0.6 fusion.6.ram
  3.7 0.7 copy.3.count
  4.4 0.7 fusion.5.sel
  5.1 0.2 fusion.13
  5.3 0.6 fusion.4.table
  5.9 135.2 %shard_map.28 = bf16[128,2,2,64,128]{4,3,2,1,0:T(8,128)(2,1)} custom-call(bf16[128,144,128]{2,1,0:T(8,128)(2,1)} %traces.1, bf16[128,160]{1,0:T(8,128)(2,1)} %fusion.5.sel, f32[128,1]{1,0:T(8,128)} %copy.3.count, bf16[128,128]{1,0:T(8,128)(2,1)} %fusion.6.ram, f32[1,128]{1,0:T(1,128)} %bitcast.3, bf16[128,128]{1,0:T(8,128)(2,1)} %fusion.4.table, ...), custom_call_target="tpu_custom_call" | custom-call | tf_op jit(solution)/shard_map/pallas_call | solution.py:300
  141.1 10.8 %copy.5 = bf16[128,2,2,64,128]{4,3,2,1,0:T(8,128)(2,1)} copy(bf16[128,2,2,64,128]{4,3,2,1,0:T(8,128)(2,1)} %shard_map.28) | data formatting | bytes 16777216
  (2 shorter events, 0.0 us)

commit v12 on v8

--- a/solution.py
+++ b/solution.py
@@ -1,5 +1,8 @@
 import functools
 import math
+
+import ml_dtypes
+import numpy as np
 
 import jax
 import jax.numpy as jnp
@@ -127,15 +130,19 @@
     inside = (outer_position >= 0) & (outer_position < total_channels)
     selector = (offset >= 0) & (offset <= 2 * halo_width) & inside[None, :]
     neighbour_count = jnp.sum(selector.astype(jnp.float32), axis=1)[:, None]
-    sample_index = jnp.arange(samples, dtype=jnp.int32)
-    ram_band = jnp.abs(sample_index[:, None] - sample_index[None, :]) <= ram_half
-    ram_count = jnp.sum(ram_band.astype(jnp.float32), axis=0)[None, :]
-    frequency = jnp.arange(1, bin_count + 1, dtype=jnp.int32)
+    sample_index = np.arange(samples, dtype=np.int32)
+    ram_band = np.abs(sample_index[:, None] - sample_index[None, :]) <= ram_half
+    ram_count = np.sum(ram_band.astype(np.float32), axis=0)[None, :]
+    frequency = np.arange(1, bin_count + 1, dtype=np.int32)
     phase_steps = frequency[:, None] * sample_index[None, :] % samples
-    phase = 2.0 * math.pi / samples * phase_steps.astype(jnp.float32)
-    dft_table = (
-        jnp.concatenate([jnp.cos(phase), -jnp.sin(phase)], axis=0) / math.sqrt(samples)
-    ).astype(jnp.bfloat16)
+    phase = np.float32(2.0 * math.pi / samples) * phase_steps.astype(np.float32)
+    dft_table = jnp.asarray(
+        (np.concatenate([np.cos(phase), -np.sin(phase)], axis=0) / np.float32(math.sqrt(samples))).astype(
+            ml_dtypes.bfloat16
+        )
+    )
+    ram_count = jnp.asarray(ram_count)
+    ram_band = jnp.asarray(ram_band)
     same_band = (bands[:, None] == bands[None, :]).astype(jnp.float32)
     band_matrix = same_band / jnp.sum(same_band, axis=1, keepdims=True)
     return [

time: 151 us -> 149 us (0.987)
  other arithmetic: 5.16 us -> 3.11 us
where the time goes in v12:
time: 149 us; the launch traced here: 146 us
  Pallas kernels  132 us (89%)
  local copies, waits for them, and re-layouts  11.5 us (8%)
  other arithmetic  3.11 us (2%)
    pallas_call x1, Pallas kernels, per_device(): pl.pallas_call(functools.partial(exchange_kernel, n, chunks, math.sqrt(wi...  132 us
    unnamed x1, local copies, waits for them, and re-layouts  10.8 us

profile of v12, /device:TPU:6, one launch (start us, length us, event | category | flops | bytes accessed | tf_op | source)
XLA Modules:
  0.0 146.3 jit_solution(8038256866456178045)
XLA Ops:
  0.0 0.9 convert_reduce_fusion.1
  0.9 0.1 convert_reduce_fusion
  1.0 1.4 convert_divide_fusion.band
  2.5 0.7 copy.6.count
  3.2 0.7 fusion.4.sel
  3.9 131.6 %shard_map.55 = bf16[128,2,2,64,128]{4,3,2,1,0:T(8,128)(2,1)} custom-call(bf16[128,144,128]{2,1,0:T(8,128)(2,1)} %traces.1, bf16[128,160]{1,0:T(8,128)(2,1)} %fusion.4.sel, f32[128,1]{1,0:T(8,128)} %copy.6.count, bf16[128,128]{1,0:T(8,128)(2,1)} %constant.28.ram, f32[1,128]{1,0:T(1,128)} %constant.25.clone.ram_count, bf16[128,128]{1,0:T(8,128)(2,1)} %constant.24.clone.table, ...), custom_call_target="tpu_custom_call" | custom-call | tf_op jit(solution)/shard_map/pallas_call | solution.py:307
  135.5 10.8 %copy.8 = bf16[128,2,2,64,128]{4,3,2,1,0:T(8,128)(2,1)} copy(bf16[128,2,2,64,128]{4,3,2,1,0:T(8,128)(2,1)} %shard_map.55) | data formatting | bytes 16777216
  (1 shorter events, 0.0 us)

commit v13 on v12

--- a/solution.py
+++ b/solution.py
@@ -196,7 +196,7 @@
         out[:, r, 1, rows, :] = jnp.stack(imag_rows, axis=1).astype(out.dtype)
 
 
-def exchange_kernel(n, chunks, scale, step, bounds, traces, sel, count, ram, ram_count, table, band,
+def exchange_kernel(n, chunks, scale, step, bounds, traces, ram, ram_count, table, band,
                     out, head, tail, owns, first, second, acc, halo_send, halo_recv,
                     first_send, first_recv, second_send, second_recv):
     me = lax.axis_index("blk")
@@ -249,7 +249,13 @@
             def _(i):
                 to_mate(owns[p], p, i).start()
 
-    consts = [r[...] for r in (sel, count, ram, ram_count, table, band)]
+    shape = (channels, channels + 2 * halo)
+    offset = lax.broadcasted_iota(jnp.int32, shape, 1) - lax.broadcasted_iota(jnp.int32, shape, 0)
+    position = me * channels - halo + lax.broadcasted_iota(jnp.int32, shape, 1)
+    inside = (position >= 0) & (position < n * channels)
+    selector = ((offset >= 0) & (offset <= 2 * halo) & inside).astype(jnp.float32)
+    count = jnp.sum(selector, axis=1, keepdims=True)
+    consts = [selector.astype(jnp.bfloat16), count] + [r[...] for r in (ram, ram_count, table, band)]
     to_right.wait_recv()
     to_left.wait_recv()
     for p, (start, length) in enumerate(bounds):
@@ -307,7 +313,7 @@
     return pl.pallas_call(
         functools.partial(exchange_kernel, n, chunks, math.sqrt(window_count), step, bounds),
         out_shape=jax.ShapeDtypeStruct((channel_count, ROUNDS, 2, bins, channel_count), jnp.bfloat16),
-        in_specs=[vmem] * 7,
+        in_specs=[vmem] * 5,
         out_specs=vmem,
         scratch_shapes=[
             pltpu.VMEM((HW, window_count, samples), jnp.bfloat16),
@@ -326,7 +332,7 @@
         compiler_params=pltpu.CompilerParams(
             collective_id=0, has_side_effects=True, vmem_limit_bytes=63 * 1024 * 1024
         ),
-    )(traces, *consts)
+    )(traces, *consts[2:])
 
 
 def solution(mesh):

time: 149 us -> 147 us (0.987)
  no operation moved by 1% of the time
where the time goes in v13:
time: 147 us; the launch traced here: 145 us
  Pallas kernels  132 us (90%)
  local copies, waits for them, and re-layouts  10.8 us (7%)
  other arithmetic  2.34 us (2%)
    pallas_call x1, Pallas kernels, per_device(): pl.pallas_call(functools.partial(exchange_kernel, n, chunks, math.sqrt(wi...  132 us
    unnamed x1, local copies, waits for them, and re-layouts  10.8 us

profile of v13, /device:TPU:6, one launch (start us, length us, event | category | flops | bytes accessed | tf_op | source)
XLA Modules:
  0.0 144.7 jit_solution(6952072704474521358)
XLA Ops:
  0.0 0.9 convert_reduce_fusion
  0.9 1.4 convert_divide_fusion.band
  2.3 131.6 %shard_map.55 = bf16[128,2,2,64,128]{4,3,2,1,0:T(8,128)(2,1)} custom-call(bf16[128,144,128]{2,1,0:T(8,128)(2,1)} %traces.1, bf16[128,128]{1,0:T(8,128)(2,1)} %constant.12.ram, f32[1,128]{1,0:T(1,128)} %constant.9.clone.ram_count, bf16[128,128]{1,0:T(8,128)(2,1)} %constant.8.clone.table, f32[64,64]{1,0:T(8,128)} %convert_divide_fusion.band), custom_call_target="tpu_custom_call" | custom-call | tf_op jit(solution)/shard_map/pallas_call | solution.py:313
  134.0 10.8 %copy.7 = bf16[128,2,2,64,128]{4,3,2,1,0:T(8,128)(2,1)} copy(bf16[128,2,2,64,128]{4,3,2,1,0:T(8,128)(2,1)} %shard_map.55) | data formatting | bytes 16777216
